TPU v7x, 128 devices: a whole 4x4x4 slice. The times are simulated.
128 devices in a mesh: gx: 16 (over z, x), gy: 4 (over y_lo, core), gz: 2 (over y_hi).
Axes of the slice: x: 4, y: 4 (y_hi: 2, y_lo: 2; y = y_hi * 2 + y_lo), z: 4, core: 2. Of those that a mesh axis runs over, the one named last changes fastest.
Arguments:
- adjoint_efield: float32 [3, 48, 128, 2048], P(None, 'gz', 'gx', 'gy'), may hold values from -6 to 6
- adjoint_hfield: float32 [3, 48, 128, 2048], P(None, 'gz', 'gx', 'gy'), may hold values from -6 to 6
- forward_efield: float32 [3, 48, 128, 2048], P(None, 'gz', 'gx', 'gy'), may hold values from -6 to 6
- material: int32 [48, 128, 2048], P('gz', 'gx', 'gy'), may hold values from 0 to 3
- permittivity: float32 [4], replicated, may hold values from 1 to 12
- design_mask: int32 [16, 256], P('gx', 'gy'), may hold values 0 or 1
- grad_sum: float32 [32, 128, 2048], P('gz', 'gx', 'gy'), may hold values from -6 to 6
Outputs:
- efield_next: float32 [3, 48, 128, 2048], P(None, 'gz', 'gx', 'gy')
- hfield_next: float32 [3, 48, 128, 2048], P(None, 'gz', 'gx', 'gy')
- grad_total: float32 [32, 128, 2048], P('gz', 'gx', 'gy')
- grad_filtered: float32 [32, 128, 2048], P('gz', 'gx', 'gy')
Inputs may be any that keep to these rules, and one draw needn't show every extreme that they name: material indices name rows of permittivity.
All inputs are finite; a program needn't handle non-finite values. No bound on the sum of `design_mask` on one device may be relied on, other than what follows from the above.
Results may differ from a plain program's by a relative error of at most 0.0003.
Values sent between devices are 32-bit elements; how exact they have to be, the bound alone decides.
A program may use at most 128 MiB of HBM per device.

v0:
```python
import functools

import jax
import jax.numpy as jnp
import numpy as np
from jax import lax
from jax.experimental import pallas as pl
from jax.experimental.pallas import tpu as pltpu
from jax.sharding import PartitionSpec as P

RADIUS = 6
BLOCK = 8
COURANT = 0.5
MESH = pl.DeviceIdType.MESH
F32 = jnp.float32
ZC = 8
PADL = 128


def cone_table():
    span = np.arange(2 * RADIUS + 1, dtype=np.float32) - np.float32(RADIUS)
    dist = np.sqrt(span[:, None] ** 2 + span[None, :] ** 2).astype(np.float32)
    cone = np.maximum(np.float32(RADIUS) - dist, np.float32(0.0))
    return (cone / cone.sum(dtype=np.float32)).astype(np.float32)


def kernel(
    sizes,
    e_hbm, h_hbm, f_hbm, m_hbm, perm_ref, mask_ref, gs_hbm,
    eo_hbm, ho_hbm, gto_hbm, gfo_hbm,
    ev, hv, fv, mv, gsv, hn, en, gt, gf,
    xu_s, xu_r, xl_s, xl_r, yu_s, yu_r, yl_s, yl_r, zu_r, zl_r,
    gsend, gmir, wide, el_s, er_s, el_r, er_r,
    in_sem, out_sem,
    xu_ss, xu_rs, xl_ss, xl_rs, yu_ss, yu_rs, yl_ss, yl_rs, z_ss, z_rs,
    m_ss, m_rs, wp_ss, wp_rs, wm_ss, wm_rs, el_ss, el_rs, er_ss, er_rs,
):
    ngx, ngy = sizes
    gx, gy, gz = lax.axis_index("gx"), lax.axis_index("gy"), lax.axis_index("gz")
    ny = hv.shape[-1]
    nchunk = m_hbm.shape[0] // (8 * ZC)
    rows = nchunk * ZC * 8
    half = ny // 2

    def dev(dx=0, dy=0):
        return {
            "gx": lax.rem(gx + (dx + ngx), ngx),
            "gy": lax.rem(gy + (dy + ngy), ngy),
            "gz": gz,
        }

    mirror = {"gx": ngx - 1 - gx, "gy": gy, "gz": gz}
    zother = {"gx": gx, "gy": gy, "gz": 1 - gz}

    def load(i, src, dst):
        c = pltpu.make_async_copy(src, dst, in_sem.at[i])
        c.start()
        return c

    tiles = ny // PADL

    def lanes(t):
        return slice(t * PADL, (t + 1) * PADL)

    def plane(ref, *at):
        lead, r = at[:-1], at[-1]
        return jnp.concatenate(
            [ref[(*lead, t, pl.ds(r, 8), slice(None))] for t in range(tiles)], 1
        )

    def put(ref, value, *at):
        lead, r = at[:-1], at[-1]
        for t in range(tiles):
            ref[(*lead, t, pl.ds(r, 8), slice(None))] = value[:, lanes(t)]

    def strided(ref, *at):
        lead, r = at[:-1], at[-1]
        return jnp.concatenate(
            [ref[(*lead, t, pl.ds(r, 8, stride=8), slice(None))] for t in range(tiles)], 1
        )

    c_e = [load(t, e_hbm.at[:, :, lanes(t)], ev.at[:, t, 0:rows, :]) for t in range(tiles)]
    c_h = load(tiles, h_hbm, hv)
    c_m = load(tiles + 1, m_hbm, mv)
    c_f = load(tiles + 2, f_hbm, fv)
    c_g = load(tiles + 3, gs_hbm, gsv)

    barrier = pltpu.get_barrier_semaphore()
    peers = [dev(dx, dy) for dx in (-1, 0, 1) for dy in (-1, 0, 1) if (dx, dy) != (0, 0)]
    peers += [mirror, zother]
    for peer in peers:
        pl.semaphore_signal(barrier, inc=1, device_id=peer, device_id_type=MESH)

    sub = lax.broadcasted_iota(jnp.int32, (8, ny), 0)
    lane = lax.broadcasted_iota(jnp.int32, (8, PADL), 1)
    zero_tile = jnp.zeros((8, PADL), F32)

    low = gz == 0
    zcs = [jnp.where(low, nchunk - 1 - k, k) for k in range(nchunk)]

    def rows_at(z):
        return pl.multiple_of(z * 8, 8)

    nblk = mask_ref.shape[1]
    spread = (
        lax.broadcasted_iota(jnp.int32, (nblk, ny), 1) // BLOCK
        == lax.broadcasted_iota(jnp.int32, (nblk, ny), 0)
    ).astype(F32)
    mask = jnp.dot(
        jnp.broadcast_to(mask_ref[...].astype(F32), (8, nblk)), spread, preferred_element_type=F32
    )
    inv = [1.0 / jnp.full((8, ny), perm_ref[i], F32) for i in range(perm_ref.shape[0])]

    def rcopy(src, dst, ss, rs, peer):
        return pltpu.make_async_remote_copy(
            src_ref=src, dst_ref=dst, send_sem=ss, recv_sem=rs, device_id=peer, device_id_type=MESH
        )

    sends = []
    for c in c_e:
        c.wait()
    xu, yu = [], []
    for k in range(nchunk):
        z0 = zcs[k] * ZC
        for i, c in enumerate((1, 2)):
            xu_s[k, i] = strided(ev, c, rows_at(z0))
        acc = zero_tile
        for j in range(ZC):
            r = rows_at(z0 + j)
            for i, c in enumerate((0, 2)):
                tile = ev[c, 0, pl.ds(r, 8), :]
                at = 32 * i + j
                acc = jnp.where(lane == at, pltpu.roll(tile, at, 1) if at else tile, acc)
        yu_s[k] = acc
    pl.semaphore_wait(barrier, len(peers))
    zu = rcopy(ev.at[0:2, :, 0:8, :], zu_r, z_ss.at[0], z_rs.at[0], zother)
    pl.when(jnp.logical_not(low))(zu.start)
    for k in range(nchunk):
        c = rcopy(yu_s.at[k], yu_r.at[k], yu_ss.at[k], yu_rs.at[k], dev(0, -1))
        c.start()
        yu.append(c)
        c = rcopy(xu_s.at[k], xu_r.at[k], xu_ss.at[k], xu_rs.at[k], dev(-1, 0))
        c.start()
        xu.append(c)
    sends += yu + xu

    c_h.wait()

    @pl.when(low)
    def _():
        zu.wait_recv()
        ev[0:2, :, rows : rows + 8, :] = zu_r[...]

    @pl.when(jnp.logical_not(low))
    def _():
        ev[0:2, :, rows : rows + 8, :] = jnp.zeros((2, tiles, 8, PADL), F32)

    xl, yl, outs = [], [], []
    zl = None
    for k in range(nchunk):
        z0 = zcs[k] * ZC
        yu[k].wait_recv()
        xu[k].wait_recv()
        ytile = jnp.where(gy == ngy - 1, 0.0, yu_r[k])
        xu_r[k] = jnp.where(gx == ngx - 1, 0.0, xu_r[k])
        acc = zero_tile
        for j in range(ZC):
            r = rows_at(z0 + j)
            ex, ey, ez = (plane(ev, c, r) for c in range(3))
            exz, eyz = (plane(ev, c, r + 8) for c in range(2))
            hx, hy, hz = (hv[c, pl.ds(r, 8), :] for c in range(3))

            def above_y(f, at):
                tile = pltpu.roll(ytile, (PADL - at) % PADL, 1) if at else ytile
                return pltpu.roll(jnp.concatenate([f, tile], 1), ny + PADL - 1, 1)[:, :ny]

            def above_x(f, i):
                row = jnp.broadcast_to(xu_r[k, i, j : j + 1, :], (8, ny))
                return jnp.where(sub == 7, row, pltpu.roll(f, 7, 0))

            exy, ezy = above_y(ex, j), above_y(ez, 32 + j)
            eyx, ezx = above_x(ey, 0), above_x(ez, 1)
            hxn = hx - COURANT * ((ezy - ez) - (eyz - ey))
            hyn = hy - COURANT * ((exz - ex) - (ezx - ez))
            hzn = hz - COURANT * ((eyx - ey) - (exy - ex))
            for c, h in enumerate((hxn, hyn, hzn)):
                put(hn, h, c, r + 8)
            for i, h in enumerate((hzn, hxn)):
                at = 32 * i + j
                rolled = pltpu.roll(h[:, ny - PADL :], at + 1, 1)
                acc = jnp.where(lane == at, rolled, acc)
        yl_s[k] = acc
        for i, c in enumerate((1, 2)):
            xl_s[k, i] = strided(hn, c, rows_at(z0 + 1) + 7)
        if k == 0:
            zl = rcopy(hn.at[0:2, :, rows : rows + 8, :], zl_r, z_ss.at[1], z_rs.at[1], zother)
        c = rcopy(yl_s.at[k], yl_r.at[k], yl_ss.at[k], yl_rs.at[k], dev(0, 1))
        c.start()
        yl.append(c)
        c = rcopy(xl_s.at[k], xl_r.at[k], xl_ss.at[k], xl_rs.at[k], dev(1, 0))
        c.start()
        xl.append(c)
        if k == 0:
            pl.when(low)(zl.start)

    sends += yl + xl
    def store(src, dst):
        c = pltpu.make_async_copy(src, dst, out_sem.at[len(outs)])
        c.start()
        outs.append(c)

    for t in range(tiles):
        store(hn.at[:, t, 8 : rows + 8, :], ho_hbm.at[:, :, lanes(t)])

    c_m.wait()
    c_f.wait()
    c_g.wait()

    @pl.when(low)
    def _():
        hn[0, :, 0:8, :] = COURANT * ev[1, :, 0:8, :]
        hn[1, :, 0:8, :] = -COURANT * ev[0, :, 0:8, :]

    @pl.when(jnp.logical_not(low))
    def _():
        zl.wait_recv()
        hn[0:2, :, 0:8, :] = zl_r[...]

    sign = jnp.where(lane < 32, COURANT, -COURANT)
    mir = []
    for k in range(nchunk):
        z0 = zcs[k] * ZC
        yl[k].wait_recv()
        xl[k].wait_recv()
        ytile = jnp.where(gy == 0, sign * yu_s[k], yl_r[k])
        xl_r[k, 0] = jnp.where(gx == 0, COURANT * xu_s[k, 1], xl_r[k, 0])
        xl_r[k, 1] = jnp.where(gx == 0, -COURANT * xu_s[k, 0], xl_r[k, 1])
        design = k < nchunk - 1
        l0 = (z0 - jnp.where(low, ZC, 0)) if design else None
        for j in range(ZC):
            r = rows_at(z0 + j)
            hx, hy, hz = (plane(hn, c, r + 8) for c in range(3))
            hxz, hyz = (plane(hn, c, r) for c in range(2))

            def below_y(f, at):
                tile = pltpu.roll(ytile, PADL - 1 - at, 1)
                return pltpu.roll(jnp.concatenate([f, tile], 1), 1, 1)[:, :ny]

            def below_x(f, i):
                row = jnp.broadcast_to(xl_r[k, i, j : j + 1, :], (8, ny))
                return jnp.where(sub == 0, row, pltpu.roll(f, 1, 0))

            hzy, hxy = below_y(hz, j), below_y(hx, 32 + j)
            hyx, hzx = below_x(hy, 0), below_x(hz, 1)
            m = mv[pl.ds(r, 8), :]
            gain = inv[-1]
            for i in range(len(inv) - 2, -1, -1):
                gain = jnp.where(m == i, inv[i], gain)
            gain = COURANT * gain
            curl = (
                (hz - hzy) - (hy - hyz),
                (hx - hxz) - (hz - hzx),
                (hy - hyx) - (hx - hxy),
            )
            dot = None
            for c in range(3):
                e = plane(ev, c, r) + gain * curl[c]
                en[c, pl.ds(r, 8), :] = e
                if design:
                    term = fv[c, pl.ds(r, 8), :] * e
                    dot = term if dot is None else dot + term
            if design:
                lr = rows_at(l0 + j)
                put(gt, gsv[pl.ds(lr, 8), :] + mask * dot, lr)
        if design:
            for x in range(8):
                gsend[k, x] = strided(gt, rows_at(l0) + x)
            for s in range(2):
                cols = slice(s * half, (s + 1) * half)
                c = rcopy(
                    gsend.at[k, :, :, cols], gmir.at[k, :, :, cols],
                    m_ss.at[k, s], m_rs.at[k, s], mirror,
                )
                c.start()
                mir.append(c)
    sends += mir
    store(en, eo_hbm)
    for t in range(tiles):
        store(gt.at[t], gto_hbm.at[:, lanes(t)])

    halo = RADIUS - 1
    nk = nchunk - 1
    wp, wm, el, er = [], [], [], []
    for k in range(nk):
        for s in range(2):
            cols = slice(s * half, (s + 1) * half)
            mir[2 * k + s].wait_recv()
            for x in range(8):
                wide[k, halo + x, :, cols] = gsend[k, x, :, cols] + gmir[k, 7 - x, :, cols]
            c = rcopy(
                wide.at[k, 8 : 8 + halo, :, cols], wide.at[k, 0:halo, :, cols],
                wp_ss.at[k, s], wp_rs.at[k, s], dev(1, 0),
            )
            c.start()
            wp.append(c)
            c = rcopy(
                wide.at[k, halo : 2 * halo, :, cols],
                wide.at[k, halo + 8 : 2 * halo + 8, :, cols],
                wm_ss.at[k, s], wm_rs.at[k, s], dev(-1, 0),
            )
            c.start()
            wm.append(c)
        left, right = zero_tile, zero_tile
        for x in range(8):
            here = (lane // 8) == x
            t = wide[k, halo + x, :, 0:PADL]
            left = jnp.where(here, pltpu.roll(t, 8 * x, 1) if x else t, left)
            t = wide[k, halo + x, :, ny - PADL : ny]
            right = jnp.where(here, pltpu.roll(t, 8 * x + 8, 1), right)
        er_s[k] = right
        el_s[k] = left
        for d in (0, 1, -1):
            c = rcopy(
                er_s.at[k], el_r.at[k, 1 - d], el_ss.at[k, 1 - d], el_rs.at[k, 1 - d], dev(d, 1)
            )
            c.start()
            el.append(c)
            c = rcopy(
                el_s.at[k], er_r.at[k, 1 - d], er_ss.at[k, 1 - d], er_rs.at[k, 1 - d], dev(d, -1)
            )
            c.start()
            er.append(c)
    sends += wp + wm + el + er

    table = cone_table()
    for k in range(nk):
        for c in el[3 * k : 3 * k + 3] + er[3 * k : 3 * k + 3]:
            c.wait_recv()
        for slot in range(3):
            gone = (gx == 0) if slot == 0 else (gx == ngx - 1)
            no_left, no_right = gy == 0, gy == ngy - 1
            if slot != 1:
                no_left, no_right = no_left | gone, no_right | gone
            tl = jnp.where(no_left, 0.0, el_r[k, slot])
            tr = jnp.where(no_right, 0.0, er_r[k, slot])
            for x in range(8):
                w = halo + x + 8 * (slot - 1)
                if 0 <= w < 8 + 2 * halo:
                    a = pltpu.roll(tl, (PADL - 8 - 8 * x) % PADL, 1)
                    b = pltpu.roll(tr, (PADL - 8 * x) % PADL, 1) if x else tr
                    wide[k, w, :, ny:] = jnp.where(lane < 64, b, a)
        for c in wp[2 * k : 2 * k + 2] + wm[2 * k : 2 * k + 2]:
            c.wait_recv()

        @pl.when(gx == 0)
        def _():
            wide[k, 0:halo, :, :ny] = jnp.zeros((halo, 8, ny), F32)

        @pl.when(gx == ngx - 1)
        def _():
            wide[k, halo + 8 :, :, :ny] = jnp.zeros((halo, 8, ny), F32)

        l0 = zcs[k] * ZC - jnp.where(low, ZC, 0)

        def row(x, carry):
            pair = [wide[k, x + halo]]
            for a in range(1, halo + 1):
                pair.append(wide[k, x + halo + a] + wide[k, x + halo - a])
            total = None
            for b in range(halo + 1):
                acc = None
                for a in range(halo + 1):
                    weight = float(table[RADIUS + a, RADIUS + b])
                    if weight > 0.0:
                        term = weight * pair[a]
                        acc = term if acc is None else acc + term
                if b == 0:
                    total = acc[:, :ny]
                else:
                    total = total + (
                        pltpu.roll(acc, b, 1)[:, :ny] + pltpu.roll(acc, ny + PADL - b, 1)[:, :ny]
                    )
            for t in range(tiles):
                gf[t, pl.ds(rows_at(l0) + x, ZC, stride=8), :] = total[:, lanes(t)]
            return carry

        lax.fori_loop(0, 8, row, 0)
        lr = rows_at(l0)
        for t in range(tiles):
            store(gf.at[t, pl.ds(lr, 8 * ZC), :], gfo_hbm.at[pl.ds(lr, 8 * ZC), lanes(t)])

    pl.when(low)(zl.wait_send)
    pl.when(jnp.logical_not(low))(zu.wait_send)
    for c in sends:
        c.wait_send()
    for c in outs:
        c.wait()


def on_device(sizes, e, h, f, material, permittivity, design_mask, grad_sum):
    nz, nx, ny = material.shape
    lay = grad_sum.shape[0]
    rows, lrows = nz * nx, lay * nx
    nchunk, nk = nz // ZC, lay // ZC
    halo, nt = RADIUS - 1, ny // PADL
    hbm = pl.BlockSpec(memory_space=pl.ANY)
    dma = pltpu.SemaphoreType.DMA
    v = lambda *shape: pltpu.VMEM(shape, F32)
    outs = pl.pallas_call(
        functools.partial(kernel, sizes),
        out_shape=(
            jax.ShapeDtypeStruct((3, rows, ny), F32),
            jax.ShapeDtypeStruct((3, rows, ny), F32),
            jax.ShapeDtypeStruct((lrows, ny), F32),
            jax.ShapeDtypeStruct((lrows, ny), F32),
        ),
        in_specs=[
            hbm, hbm, hbm, hbm,
            pl.BlockSpec(memory_space=pltpu.SMEM),
            pl.BlockSpec(memory_space=pltpu.VMEM),
            hbm,
        ],
        out_specs=(hbm, hbm, hbm, hbm),
        scratch_shapes=[
            v(3, nt, rows + 8, PADL),
            v(3, rows, ny),
            v(3, rows, ny),
            pltpu.VMEM((rows, ny), jnp.int32),
            v(lrows, ny),
            v(3, nt, rows + 8, PADL),
            v(3, rows, ny),
            v(nt, lrows, PADL),
            v(nt, lrows, PADL),
            v(nchunk, 2, ZC, ny), v(nchunk, 2, ZC, ny),
            v(nchunk, 2, ZC, ny), v(nchunk, 2, ZC, ny),
            v(nchunk, 8, PADL), v(nchunk, 8, PADL),
            v(nchunk, 8, PADL), v(nchunk, 8, PADL),
            v(2, nt, 8, PADL), v(2, nt, 8, PADL),
            v(nk, 8, ZC, ny), v(nk, 8, ZC, ny),
            v(nk, 8 + 2 * halo, ZC, ny + PADL),
            v(nk, 8, PADL), v(nk, 8, PADL),
            v(nk, 3, 8, PADL), v(nk, 3, 8, PADL),
            dma((nt + 4,)), dma((2 * nt + 1 + nk * nt,)),
            dma((nchunk,)), dma((nchunk,)), dma((nchunk,)), dma((nchunk,)),
            dma((nchunk,)), dma((nchunk,)), dma((nchunk,)), dma((nchunk,)),
            dma((2,)), dma((2,)),
            dma((nk, 2)), dma((nk, 2)), dma((nk, 2)), dma((nk, 2)), dma((nk, 2)), dma((nk, 2)),
            dma((nk, 3)), dma((nk, 3)), dma((nk, 3)), dma((nk, 3)),
        ],
        compiler_params=pltpu.CompilerParams(
            collective_id=0, has_side_effects=True, vmem_limit_bytes=48 * 1024 * 1024
        ),
    )(
        e.reshape(3, rows, ny), h.reshape(3, rows, ny), f.reshape(3, rows, ny),
        material.reshape(rows, ny), permittivity, design_mask, grad_sum.reshape(lrows, ny),
    )
    return (
        outs[0].reshape(3, nz, nx, ny),
        outs[1].reshape(3, nz, nx, ny),
        outs[2].reshape(lay, nx, ny),
        outs[3].reshape(lay, nx, ny),
    )


def solution(mesh):
    field = P(None, "gz", "gx", "gy")
    cells = P("gz", "gx", "gy")
    return jax.shard_map(
        functools.partial(on_device, (mesh.shape["gx"], mesh.shape["gy"])),
        mesh=mesh,
        in_specs=(field, field, field, cells, P(), P("gx", "gy"), cells),
        out_specs=(field, field, cells, cells),
        check_vma=False,
    )
```

profile of v0, /device:TPU:1, one launch (start us, length us, event | category | flops | bytes accessed | tf_op | source)
XLA Modules:
  0.0 45.4 jit_solution(18049521061828047114)
XLA Ops:
  0.6 0.0 copy-start
  0.6 1.3 %copy-done = f32[3,24,8,512]{3,2,1,0:T(8,128)S(1)} copy-done((f32[3,24,8,512]{3,2,1,0:T(8,128)S(1)}, f32[3,24,8,512]{3,2,1,0:T(8,128)}, u32[]{:S(2)}) %copy-start) | copy-done | bytes 1179672
  1.9 0.0 copy-start.1
  1.9 1.3 %copy-done.1 = f32[3,24,8,512]{3,2,1,0:T(8,128)S(1)} copy-done((f32[3,24,8,512]{3,2,1,0:T(8,128)S(1)}, f32[3,24,8,512]{3,2,1,0:T(8,128)}, u32[]{:S(2)}) %copy-start.1) | copy-done | bytes 1179672
  3.2 0.0 copy-start.2
  3.2 1.0 %copy-done.2 = s32[24,8,512]{2,1,0:T(8,128)S(1)} copy-done((s32[24,8,512]{2,1,0:T(8,128)S(1)}, s32[24,8,512]{2,1,0:T(8,128)}, u32[]{:S(2)}) %copy-start.2) | copy-done | bytes 393240
  4.2 0.0 copy-start.3
  4.2 0.9 %copy-done.3 = f32[16,8,512]{2,1,0:T(8,128)S(1)} copy-done((f32[16,8,512]{2,1,0:T(8,128)S(1)}, f32[16,8,512]{2,1,0:T(8,128)}, u32[]{:S(2)}) %copy-start.3) | copy-done | bytes 262168
  5.1 0.0 copy-start.4
  5.1 0.7 %copy-done.4 = f32[4]{0:T(128)S(1)} copy-done((f32[4]{0:T(128)S(1)}, f32[4]{0:T(128)}, u32[]{:S(2)}) %copy-start.4) | copy-done | bytes 40
  5.8 0.0 copy-start.5
  5.8 0.7 %copy-done.5 = s32[1,64]{1,0:T(1,128)S(1)} copy-done((s32[1,64]{1,0:T(1,128)S(1)}, s32[1,64]{1,0:T(1,128)}, u32[]{:S(2)}) %copy-start.5) | copy-done | bytes 280
  6.4 35.6 %shard_map.102 = (f32[3,192,512]{2,1,0:T(8,128)S(1)}, f32[3,192,512]{2,1,0:T(8,128)S(1)}, f32[128,512]{1,0:T(8,128)S(1)}, f32[128,512]{1,0:T(8,128)S(1)}) custom-call(f32[3,192,512]{2,1,0:T(8,128)S(1)} %bitcast.9, f32[3,192,512]{2,1,0:T(8,128)S(1)} %bitcast.10, f32[3,192,512]{2,1,0:T(8,128)} %bitcast.17, s32[192,512]{1,0:T(8,128)S(1)} %bitcast.13, ...), custom_call_target="tpu_custom_call" | custom-call | tf_op jit(solution)/shard_map/pallas_call | solution.py:409
  42.0 1.0 %copy.15 = f32[3,24,8,512]{3,2,1,0:T(8,128)} copy(f32[3,24,8,512]{3,2,1,0:T(8,128)S(1)} %bitcast.12) | data formatting | bytes 2359296
  43.0 1.0 %copy.16 = f32[3,24,8,512]{3,2,1,0:T(8,128)} copy(f32[3,24,8,512]{3,2,1,0:T(8,128)S(1)} %bitcast.11) | data formatting | bytes 2359296
  44.0 0.7 %copy.17 = f32[16,8,512]{2,1,0:T(8,128)} copy(f32[16,8,512]{2,1,0:T(8,128)S(1)} %bitcast.16) | data formatting | bytes 524288
  44.7 0.7 %copy.18 = f32[16,8,512]{2,1,0:T(8,128)} copy(f32[16,8,512]{2,1,0:T(8,128)S(1)} %bitcast.15) | data formatting | bytes 524288
Async XLA Ops:
  0.6 1.3 %copy-start = (f32[3,24,8,512]{3,2,1,0:T(8,128)S(1)}, f32[3,24,8,512]{3,2,1,0:T(8,128)}, u32[]{:S(2)}) copy-start(f32[3,24,8,512]{3,2,1,0:T(8,128)} %param.7) | copy-start | bytes 3538948
  1.9 1.3 %copy-start.1 = (f32[3,24,8,512]{3,2,1,0:T(8,128)S(1)}, f32[3,24,8,512]{3,2,1,0:T(8,128)}, u32[]{:S(2)}) copy-start(f32[3,24,8,512]{3,2,1,0:T(8,128)} %param.8) | copy-start | bytes 3538948
  3.2 1.0 %copy-start.2 = (s32[24,8,512]{2,1,0:T(8,128)S(1)}, s32[24,8,512]{2,1,0:T(8,128)}, u32[]{:S(2)}) copy-start(s32[24,8,512]{2,1,0:T(8,128)} %param.10) | copy-start | bytes 1179652
  4.2 0.9 %copy-start.3 = (f32[16,8,512]{2,1,0:T(8,128)S(1)}, f32[16,8,512]{2,1,0:T(8,128)}, u32[]{:S(2)}) copy-start(f32[16,8,512]{2,1,0:T(8,128)} %param.13) | copy-start | bytes 786436
  5.1 0.7 %copy-start.4 = (f32[4]{0:T(128)S(1)}, f32[4]{0:T(128)}, u32[]{:S(2)}) copy-start(f32[4]{0:T(128)} %perm_ref.1) | copy-start | bytes 52
  5.8 0.7 %copy-start.5 = (s32[1,64]{1,0:T(1,128)S(1)}, s32[1,64]{1,0:T(1,128)}, u32[]{:S(2)}) copy-start(s32[1,64]{1,0:T(1,128)} %mask_ref.1) | copy-start | bytes 772
where the time goes:
time: 45.7 us; the launch traced here: 45.4 us
  Pallas kernels  35.6 us (78%)
  local copies, waits for them, and re-layouts  9.22 us (20%)
  between operations  0.66 us (1%)
    pallas_call x1, Pallas kernels, on_device(): pl.pallas_call(functools.partial(kernel, sizes), out_shape=(jax.ShapeDtyp...  35.6 us
    unnamed x16, local copies, waits for them, and re-layouts  9.22 us

commit v1 on v0

--- a/solution.py
+++ b/solution.py
@@ -27,13 +27,14 @@
 def kernel(
     sizes,
     e_hbm, h_hbm, f_hbm, m_hbm, perm_ref, mask_ref, gs_hbm,
-    eo_hbm, ho_hbm, gto_hbm, gfo_hbm,
-    ev, hv, fv, mv, gsv, hn, en, gt, gf,
+    en, hn, gt, gf, last,
+    ev, hv, fv, mv, gsv,
     xu_s, xu_r, xl_s, xl_r, yu_s, yu_r, yl_s, yl_r, zu_r, zl_r,
-    gsend, gmir, wide, el_s, er_s, el_r, er_r,
-    in_sem, out_sem,
+    gsend, gmir, wide, el_s, er_s, el_r, er_r, q_s, q_m, sq, sq_p, sq_n,
+    in_sem,
     xu_ss, xu_rs, xl_ss, xl_rs, yu_ss, yu_rs, yl_ss, yl_rs, z_ss, z_rs,
     m_ss, m_rs, wp_ss, wp_rs, wm_ss, wm_rs, el_ss, el_rs, er_ss, er_rs,
+    q_ss, q_rs, sp_ss, sp_rs, sn_ss, sn_rs,
 ):
     ngx, ngy = sizes
     gx, gy, gz = lax.axis_index("gx"), lax.axis_index("gy"), lax.axis_index("gz")
@@ -86,8 +87,7 @@
     c_g = load(tiles + 3, gs_hbm, gsv)
 
     barrier = pltpu.get_barrier_semaphore()
-    peers = [dev(dx, dy) for dx in (-1, 0, 1) for dy in (-1, 0, 1) if (dx, dy) != (0, 0)]
-    peers += [mirror, zother]
+    peers = [dev(-1, 0), dev(1, 0), dev(0, -1), dev(0, 1), mirror, zother]
     for peer in peers:
         pl.semaphore_signal(barrier, inc=1, device_id=peer, device_id_type=MESH)
 
@@ -155,7 +155,7 @@
     def _():
         ev[0:2, :, rows : rows + 8, :] = jnp.zeros((2, tiles, 8, PADL), F32)
 
-    xl, yl, outs = [], [], []
+    xl, yl = [], []
     zl = None
     for k in range(nchunk):
         z0 = zcs[k] * ZC
@@ -204,13 +204,6 @@
             pl.when(low)(zl.start)
 
     sends += yl + xl
-    def store(src, dst):
-        c = pltpu.make_async_copy(src, dst, out_sem.at[len(outs)])
-        c.start()
-        outs.append(c)
-
-    for t in range(tiles):
-        store(hn.at[:, t, 8 : rows + 8, :], ho_hbm.at[:, :, lanes(t)])
 
     c_m.wait()
     c_f.wait()
@@ -227,7 +220,7 @@
         hn[0:2, :, 0:8, :] = zl_r[...]
 
     sign = jnp.where(lane < 32, COURANT, -COURANT)
-    mir = []
+    mir, el, er, qm = [], [], [], []
     for k in range(nchunk):
         z0 = zcs[k] * ZC
         yl[k].wait_recv()
@@ -273,8 +266,22 @@
                 lr = rows_at(l0 + j)
                 put(gt, gsv[pl.ds(lr, 8), :] + mask * dot, lr)
         if design:
+            left, right = zero_tile, zero_tile
             for x in range(8):
-                gsend[k, x] = strided(gt, rows_at(l0) + x)
+                g = strided(gt, rows_at(l0) + x)
+                gsend[k, x] = g
+                here = (lane // 8) == x
+                t = g[:, :PADL]
+                left = jnp.where(here, pltpu.roll(t, 8 * x, 1) if x else t, left)
+                right = jnp.where(here, pltpu.roll(g[:, ny - PADL :], 8 * x + 8, 1), right)
+            er_s[k] = right
+            el_s[k] = left
+            c = rcopy(er_s.at[k], el_r.at[k], el_ss.at[k], el_rs.at[k], dev(0, 1))
+            c.start()
+            el.append(c)
+            c = rcopy(el_s.at[k], er_r.at[k], er_ss.at[k], er_rs.at[k], dev(0, -1))
+            c.start()
+            er.append(c)
             for s in range(2):
                 cols = slice(s * half, (s + 1) * half)
                 c = rcopy(
@@ -283,15 +290,33 @@
                 )
                 c.start()
                 mir.append(c)
-    sends += mir
-    store(en, eo_hbm)
-    for t in range(tiles):
-        store(gt.at[t], gto_hbm.at[:, lanes(t)])
+    for k in range(nchunk - 1):
+        el[k].wait_recv()
+        er[k].wait_recv()
+        beyond_left = jnp.where(gy == 0, 0.0, el_r[k])
+        beyond_right = jnp.where(gy == ngy - 1, 0.0, er_r[k])
+        q_s[k] = jnp.where(lane < 64, beyond_left, pltpu.roll(beyond_right, 64, 1))
+        c = rcopy(q_s.at[k], q_m.at[k], q_ss.at[k], q_rs.at[k], mirror)
+        c.start()
+        qm.append(c)
+    sends += mir + el + er + qm
 
     halo = RADIUS - 1
     nk = nchunk - 1
-    wp, wm, el, er = [], [], [], []
+    wp, wm, sp, sn = [], [], [], []
     for k in range(nk):
+        qm[k].wait_recv()
+        flipped = zero_tile
+        for x in range(8):
+            here = ((lane // 8) % 8) == x
+            flipped = jnp.where(here, pltpu.roll(q_m[k], (8 * (2 * x - 7)) % PADL, 1), flipped)
+        sq[k] = q_s[k] + flipped
+        c = rcopy(sq.at[k], sq_p.at[k], sp_ss.at[k], sp_rs.at[k], dev(1, 0))
+        c.start()
+        sp.append(c)
+        c = rcopy(sq.at[k], sq_n.at[k], sn_ss.at[k], sn_rs.at[k], dev(-1, 0))
+        c.start()
+        sn.append(c)
         for s in range(2):
             cols = slice(s * half, (s + 1) * half)
             mir[2 * k + s].wait_recv()
@@ -310,45 +335,21 @@
             )
             c.start()
             wm.append(c)
-        left, right = zero_tile, zero_tile
-        for x in range(8):
-            here = (lane // 8) == x
-            t = wide[k, halo + x, :, 0:PADL]
-            left = jnp.where(here, pltpu.roll(t, 8 * x, 1) if x else t, left)
-            t = wide[k, halo + x, :, ny - PADL : ny]
-            right = jnp.where(here, pltpu.roll(t, 8 * x + 8, 1), right)
-        er_s[k] = right
-        el_s[k] = left
-        for d in (0, 1, -1):
-            c = rcopy(
-                er_s.at[k], el_r.at[k, 1 - d], el_ss.at[k, 1 - d], el_rs.at[k, 1 - d], dev(d, 1)
-            )
-            c.start()
-            el.append(c)
-            c = rcopy(
-                el_s.at[k], er_r.at[k, 1 - d], er_ss.at[k, 1 - d], er_rs.at[k, 1 - d], dev(d, -1)
-            )
-            c.start()
-            er.append(c)
-    sends += wp + wm + el + er
-
-    table = cone_table()
+    sends += wp + wm + sp + sn
+
     for k in range(nk):
-        for c in el[3 * k : 3 * k + 3] + er[3 * k : 3 * k + 3]:
-            c.wait_recv()
-        for slot in range(3):
-            gone = (gx == 0) if slot == 0 else (gx == ngx - 1)
-            no_left, no_right = gy == 0, gy == ngy - 1
-            if slot != 1:
-                no_left, no_right = no_left | gone, no_right | gone
-            tl = jnp.where(no_left, 0.0, el_r[k, slot])
-            tr = jnp.where(no_right, 0.0, er_r[k, slot])
-            for x in range(8):
-                w = halo + x + 8 * (slot - 1)
-                if 0 <= w < 8 + 2 * halo:
-                    a = pltpu.roll(tl, (PADL - 8 - 8 * x) % PADL, 1)
-                    b = pltpu.roll(tr, (PADL - 8 * x) % PADL, 1) if x else tr
-                    wide[k, w, :, ny:] = jnp.where(lane < 64, b, a)
+        sp[k].wait_recv()
+        sn[k].wait_recv()
+        packs = (
+            jnp.where(gx == 0, 0.0, sq_p[k]),
+            sq[k],
+            jnp.where(gx == ngx - 1, 0.0, sq_n[k]),
+        )
+        for w in range(8 + 2 * halo):
+            slot, x = (w - halo + 8) // 8, (w - halo) % 8
+            a = pltpu.roll(packs[slot], (PADL - 8 - 8 * x) % PADL, 1)
+            b = pltpu.roll(packs[slot], 64 - 8 * x, 1)
+            wide[k, w, :, ny:] = jnp.where(lane < 64, b, a)
         for c in wp[2 * k : 2 * k + 2] + wm[2 * k : 2 * k + 2]:
             c.wait_recv()
 
@@ -360,39 +361,69 @@
         def _():
             wide[k, halo + 8 :, :, :ny] = jnp.zeros((halo, 8, ny), F32)
 
-        l0 = zcs[k] * ZC - jnp.where(low, ZC, 0)
-
-        def row(x, carry):
-            pair = [wide[k, x + halo]]
-            for a in range(1, halo + 1):
-                pair.append(wide[k, x + halo + a] + wide[k, x + halo - a])
-            total = None
-            for b in range(halo + 1):
-                acc = None
-                for a in range(halo + 1):
-                    weight = float(table[RADIUS + a, RADIUS + b])
-                    if weight > 0.0:
-                        term = weight * pair[a]
-                        acc = term if acc is None else acc + term
-                if b == 0:
-                    total = acc[:, :ny]
-                else:
-                    total = total + (
-                        pltpu.roll(acc, b, 1)[:, :ny] + pltpu.roll(acc, ny + PADL - b, 1)[:, :ny]
-                    )
-            for t in range(tiles):
-                gf[t, pl.ds(rows_at(l0) + x, ZC, stride=8), :] = total[:, lanes(t)]
-            return carry
-
-        lax.fori_loop(0, 8, row, 0)
-        lr = rows_at(l0)
-        for t in range(tiles):
-            store(gf.at[t, pl.ds(lr, 8 * ZC), :], gfo_hbm.at[pl.ds(lr, 8 * ZC), lanes(t)])
+        if k < nk - 1:
+            smooth(wide.at[k], gf)
+        else:
+            last[...] = wide[k]
 
     pl.when(low)(zl.wait_send)
     pl.when(jnp.logical_not(low))(zu.wait_send)
     for c in sends:
         c.wait_send()
+
+
+def smooth(rows_ref, out_ref):
+    table = cone_table()
+    halo, tiles = RADIUS - 1, out_ref.shape[0]
+    ny = tiles * PADL
+
+    def row(x, carry):
+        pair = [rows_ref[x + halo]]
+        for a in range(1, halo + 1):
+            pair.append(rows_ref[x + halo + a] + rows_ref[x + halo - a])
+        total = None
+        for b in range(halo + 1):
+            acc = None
+            for a in range(halo + 1):
+                weight = float(table[RADIUS + a, RADIUS + b])
+                if weight > 0.0:
+                    term = weight * pair[a]
+                    acc = term if acc is None else acc + term
+            if b == 0:
+                total = acc[:, :ny]
+            else:
+                total = total + (
+                    pltpu.roll(acc, b, 1)[:, :ny] + pltpu.roll(acc, ny + PADL - b, 1)[:, :ny]
+                )
+        for t in range(tiles):
+            out_ref[t, pl.ds(x, ZC, stride=8), :] = total[:, t * PADL : (t + 1) * PADL]
+        return carry
+
+    lax.fori_loop(0, 8, row, 0)
+
+
+def finish(en, hn, gt, gf, last, eo, ho, gto, gfo, gl, sem):
+    tiles, rows = gt.shape[0], en.shape[1]
+    low = lax.axis_index("gz") == 0
+    outs = []
+
+    def store(src, dst):
+        c = pltpu.make_async_copy(src, dst, sem.at[len(outs)])
+        c.start()
+        outs.append(c)
+
+    n = 8 * ZC
+    first = pl.multiple_of(jnp.where(low, n, 0), n)
+    store(en, eo)
+    for t in range(tiles):
+        cols = slice(t * PADL, (t + 1) * PADL)
+        store(hn.at[:, t, 8 : rows + 8, :], ho.at[:, :, cols])
+        store(gt.at[t], gto.at[:, cols])
+        store(gf.at[t], gfo.at[pl.ds(first, n), cols])
+    smooth(last, gl)
+    for t in range(tiles):
+        cols = slice(t * PADL, (t + 1) * PADL)
+        store(gl.at[t], gfo.at[pl.ds(n - first, n), cols])
     for c in outs:
         c.wait()
 
@@ -403,16 +434,18 @@
     rows, lrows = nz * nx, lay * nx
     nchunk, nk = nz // ZC, lay // ZC
     halo, nt = RADIUS - 1, ny // PADL
-    hbm = pl.BlockSpec(memory_space=pl.ANY)
+    hbm = pl.BlockSpec(memory_space=pltpu.HBM)
+    vmem = pl.BlockSpec(memory_space=pltpu.VMEM)
     dma = pltpu.SemaphoreType.DMA
     v = lambda *shape: pltpu.VMEM(shape, F32)
-    outs = pl.pallas_call(
+    mid = pl.pallas_call(
         functools.partial(kernel, sizes),
         out_shape=(
-            jax.ShapeDtypeStruct((3, rows, ny), F32),
-            jax.ShapeDtypeStruct((3, rows, ny), F32),
-            jax.ShapeDtypeStruct((lrows, ny), F32),
-            jax.ShapeDtypeStruct((lrows, ny), F32),
+            v(3, rows, ny),
+            v(3, nt, rows + 8, PADL),
+            v(nt, lrows, PADL),
+            v(nt, 8 * ZC, PADL),
+            v(8 + 2 * halo, ZC, ny + PADL),
         ),
         in_specs=[
             hbm, hbm, hbm, hbm,
@@ -420,17 +453,13 @@
             pl.BlockSpec(memory_space=pltpu.VMEM),
             hbm,
         ],
-        out_specs=(hbm, hbm, hbm, hbm),
+        out_specs=(vmem,) * 5,
         scratch_shapes=[
             v(3, nt, rows + 8, PADL),
             v(3, rows, ny),
             v(3, rows, ny),
             pltpu.VMEM((rows, ny), jnp.int32),
             v(lrows, ny),
-            v(3, nt, rows + 8, PADL),
-            v(3, rows, ny),
-            v(nt, lrows, PADL),
-            v(nt, lrows, PADL),
             v(nchunk, 2, ZC, ny), v(nchunk, 2, ZC, ny),
             v(nchunk, 2, ZC, ny), v(nchunk, 2, ZC, ny),
             v(nchunk, 8, PADL), v(nchunk, 8, PADL),
@@ -439,21 +468,36 @@
             v(nk, 8, ZC, ny), v(nk, 8, ZC, ny),
             v(nk, 8 + 2 * halo, ZC, ny + PADL),
             v(nk, 8, PADL), v(nk, 8, PADL),
-            v(nk, 3, 8, PADL), v(nk, 3, 8, PADL),
-            dma((nt + 4,)), dma((2 * nt + 1 + nk * nt,)),
+            v(nk, 8, PADL), v(nk, 8, PADL),
+            v(nk, 8, PADL), v(nk, 8, PADL), v(nk, 8, PADL), v(nk, 8, PADL), v(nk, 8, PADL),
+            dma((nt + 4,)),
             dma((nchunk,)), dma((nchunk,)), dma((nchunk,)), dma((nchunk,)),
             dma((nchunk,)), dma((nchunk,)), dma((nchunk,)), dma((nchunk,)),
             dma((2,)), dma((2,)),
             dma((nk, 2)), dma((nk, 2)), dma((nk, 2)), dma((nk, 2)), dma((nk, 2)), dma((nk, 2)),
-            dma((nk, 3)), dma((nk, 3)), dma((nk, 3)), dma((nk, 3)),
+            dma((nk,)), dma((nk,)), dma((nk,)), dma((nk,)),
+            dma((nk,)), dma((nk,)), dma((nk,)), dma((nk,)), dma((nk,)), dma((nk,)),
         ],
         compiler_params=pltpu.CompilerParams(
-            collective_id=0, has_side_effects=True, vmem_limit_bytes=48 * 1024 * 1024
+            collective_id=0, has_side_effects=True, vmem_limit_bytes=63_500_000
         ),
     )(
         e.reshape(3, rows, ny), h.reshape(3, rows, ny), f.reshape(3, rows, ny),
         material.reshape(rows, ny), permittivity, design_mask, grad_sum.reshape(lrows, ny),
     )
+    outs = pl.pallas_call(
+        finish,
+        out_shape=(
+            jax.ShapeDtypeStruct((3, rows, ny), F32),
+            jax.ShapeDtypeStruct((3, rows, ny), F32),
+            jax.ShapeDtypeStruct((lrows, ny), F32),
+            jax.ShapeDtypeStruct((lrows, ny), F32),
+        ),
+        in_specs=[vmem] * 5,
+        out_specs=(hbm,) * 4,
+        scratch_shapes=[v(nt, 8 * ZC, PADL), dma((1 + 4 * nt,))],
+        compiler_params=pltpu.CompilerParams(vmem_limit_bytes=32 * 1024 * 1024),
+    )(*mid)
     return (
         outs[0].reshape(3, nz, nx, ny),
         outs[1].reshape(3, nz, nx, ny),

time: 45.7 us -> 35 us (0.77)
  local copies, waits for them, and re-layouts: 9.22 us -> 0 us
  Pallas kernels: 35.6 us -> 34.2 us
    unnamed x16 -> x0, local copies, waits for them, and re-layouts: 9.22 us -> none
    pallas_call x1 -> x2, Pallas kernels: 35.6 us -> 34.2 us  [the longest x1 32.3 us: on_device(): pl.pallas_call(functools.partial(kernel, sizes), out_shape=(v(3, rows, ny...]
where the time goes in v1:
time: 35 us; the launch traced here: 34.9 us
  Pallas kernels  34.2 us (98%)
  between operations  0.64 us (2%)
    pallas_call x1, Pallas kernels, on_device(): pl.pallas_call(functools.partial(kernel, sizes), out_shape=(v(3, rows, ny...  32.3 us
    pallas_call x1, Pallas kernels, on_device(): pl.pallas_call(finish, out_shape=(jax.ShapeDtypeStruct((3, rows, ny), F32...  1.92 us

profile of v1, /device:TPU:1, one launch (start us, length us, event | category | flops | bytes accessed | tf_op | source)
XLA Modules:
  0.0 34.9 jit_solution(17422121344730626401)
XLA Ops:
  0.6 32.3 %shard_map.102 = (f32[3,192,512]{2,1,0:T(8,128)S(1)}, f32[3,4,200,128]{3,2,1,0:T(8,128)S(1)}, f32[4,128,128]{2,1,0:T(8,128)S(1)}, f32[4,64,128]{2,1,0:T(8,128)S(1)}, f32[18,8,640]{2,1,0:T(8,128)S(1)}) custom-call(f32[3,192,512]{2,1,0:T(8,128)} %bitcast.9, f32[3,192,512]{2,1,0:T(8,128)} %bitcast.10, f32[3,192,512]{2,1,0:T(8,128)} %bitcast.11, ...), custom_call_target="tpu_custom_call" | custom-call | tf_op jit(solution)/shard_map/pallas_call | solution.py:441
  32.9 1.9 %shard_map.103 = (f32[3,192,512]{2,1,0:T(8,128)}, f32[3,192,512]{2,1,0:T(8,128)}, f32[128,512]{1,0:T(8,128)}, f32[128,512]{1,0:T(8,128)}) custom-call(f32[3,192,512]{2,1,0:T(8,128)S(1)} %get-tuple-element.13.en, f32[3,4,200,128]{3,2,1,0:T(8,128)S(1)} %get-tuple-element.14.hn, f32[4,128,128]{2,1,0:T(8,128)S(1)} %get-tuple-element.15.gt, ...), custom_call_target="tpu_custom_call" | custom-call | tf_op jit(solution)/shard_map/pallas_call | solution.py:488

commit v2 on v1

--- a/solution.py
+++ b/solution.py
@@ -26,11 +26,11 @@
 
 def kernel(
     sizes,
-    e_hbm, h_hbm, f_hbm, m_hbm, perm_ref, mask_ref, gs_hbm,
+    e_hbm, h_hbm, f_hbm, m_hbm, perm_hbm, mask_hbm, gs_hbm,
     en, hn, gt, gf, last,
-    ev, hv, fv, mv, gsv,
+    ev, hv, fv, mv, gsv, perm_ref, mask_ref,
     xu_s, xu_r, xl_s, xl_r, yu_s, yu_r, yl_s, yl_r, zu_r, zl_r,
-    gsend, gmir, wide, el_s, er_s, el_r, er_r, q_s, q_m, sq, sq_p, sq_n,
+    gsend, gmir, wide, el_s, er_s, el_r, er_r, q_s, q_m, sq, sq_p, sq_n, turned,
     in_sem,
     xu_ss, xu_rs, xl_ss, xl_rs, yu_ss, yu_rs, yl_ss, yl_rs, z_ss, z_rs,
     m_ss, m_rs, wp_ss, wp_rs, wm_ss, wm_rs, el_ss, el_rs, er_ss, er_rs,
@@ -53,6 +53,22 @@
     mirror = {"gx": ngx - 1 - gx, "gy": gy, "gz": gz}
     zother = {"gx": gx, "gy": gy, "gz": 1 - gz}
 
+    even = lax.rem(gx, 2) == 0
+    image_at = jnp.where(even, ngx, ngx - 2) - gx
+    own_image = image_at == gx
+    has_image = (gx != 0) & (gx != ngx - 1) & jnp.logical_not(own_image)
+    image = {"gx": lax.rem(image_at + ngx, ngx), "gy": gy, "gz": gz}
+
+    barrier = pltpu.get_barrier_semaphore()
+    peers = [dev(-1, 0), dev(1, 0), dev(0, -1), dev(0, 1), mirror, zother]
+    for peer in peers:
+        pl.semaphore_signal(barrier, inc=1, device_id=peer, device_id_type=MESH)
+
+    @pl.when(has_image)
+    def _():
+        pl.semaphore_signal(barrier, inc=1, device_id=image, device_id_type=MESH)
+
+
     def load(i, src, dst):
         c = pltpu.make_async_copy(src, dst, in_sem.at[i])
         c.start()
@@ -84,12 +100,9 @@
     c_h = load(tiles, h_hbm, hv)
     c_m = load(tiles + 1, m_hbm, mv)
     c_f = load(tiles + 2, f_hbm, fv)
+    c_p = load(tiles + 4, perm_hbm, perm_ref)
+    c_k = load(tiles + 5, mask_hbm, mask_ref)
     c_g = load(tiles + 3, gs_hbm, gsv)
-
-    barrier = pltpu.get_barrier_semaphore()
-    peers = [dev(-1, 0), dev(1, 0), dev(0, -1), dev(0, 1), mirror, zother]
-    for peer in peers:
-        pl.semaphore_signal(barrier, inc=1, device_id=peer, device_id_type=MESH)
 
     sub = lax.broadcasted_iota(jnp.int32, (8, ny), 0)
     lane = lax.broadcasted_iota(jnp.int32, (8, PADL), 1)
@@ -100,16 +113,6 @@
 
     def rows_at(z):
         return pl.multiple_of(z * 8, 8)
-
-    nblk = mask_ref.shape[1]
-    spread = (
-        lax.broadcasted_iota(jnp.int32, (nblk, ny), 1) // BLOCK
-        == lax.broadcasted_iota(jnp.int32, (nblk, ny), 0)
-    ).astype(F32)
-    mask = jnp.dot(
-        jnp.broadcast_to(mask_ref[...].astype(F32), (8, nblk)), spread, preferred_element_type=F32
-    )
-    inv = [1.0 / jnp.full((8, ny), perm_ref[i], F32) for i in range(perm_ref.shape[0])]
 
     def rcopy(src, dst, ss, rs, peer):
         return pltpu.make_async_remote_copy(
@@ -119,7 +122,7 @@
     sends = []
     for c in c_e:
         c.wait()
-    xu, yu = [], []
+    xu = []
     for k in range(nchunk):
         z0 = zcs[k] * ZC
         for i, c in enumerate((1, 2)):
@@ -132,17 +135,28 @@
                 at = 32 * i + j
                 acc = jnp.where(lane == at, pltpu.roll(tile, at, 1) if at else tile, acc)
         yu_s[k] = acc
-    pl.semaphore_wait(barrier, len(peers))
+    pl.semaphore_wait(barrier, len(peers) + has_image.astype(jnp.int32))
+    yu = rcopy(yu_s, yu_r, yu_ss.at[0], yu_rs.at[0], dev(0, -1))
+    yu.start()
     zu = rcopy(ev.at[0:2, :, 0:8, :], zu_r, z_ss.at[0], z_rs.at[0], zother)
     pl.when(jnp.logical_not(low))(zu.start)
     for k in range(nchunk):
-        c = rcopy(yu_s.at[k], yu_r.at[k], yu_ss.at[k], yu_rs.at[k], dev(0, -1))
-        c.start()
-        yu.append(c)
         c = rcopy(xu_s.at[k], xu_r.at[k], xu_ss.at[k], xu_rs.at[k], dev(-1, 0))
         c.start()
         xu.append(c)
-    sends += yu + xu
+    sends += [yu] + xu
+
+    c_p.wait()
+    c_k.wait()
+    nblk = mask_ref.shape[1]
+    spread = (
+        lax.broadcasted_iota(jnp.int32, (nblk, ny), 1) // BLOCK
+        == lax.broadcasted_iota(jnp.int32, (nblk, ny), 0)
+    ).astype(F32)
+    mask = jnp.dot(
+        jnp.broadcast_to(mask_ref[...].astype(F32), (8, nblk)), spread, preferred_element_type=F32
+    )
+    inv = [1.0 / jnp.full((8, ny), perm_ref[i], F32) for i in range(perm_ref.shape[0])]
 
     c_h.wait()
 
@@ -159,7 +173,8 @@
     zl = None
     for k in range(nchunk):
         z0 = zcs[k] * ZC
-        yu[k].wait_recv()
+        if k == 0:
+            yu.wait_recv()
         xu[k].wait_recv()
         ytile = jnp.where(gy == ngy - 1, 0.0, yu_r[k])
         xu_r[k] = jnp.where(gx == ngx - 1, 0.0, xu_r[k])
@@ -322,20 +337,44 @@
             mir[2 * k + s].wait_recv()
             for x in range(8):
                 wide[k, halo + x, :, cols] = gsend[k, x, :, cols] + gmir[k, 7 - x, :, cols]
-            c = rcopy(
-                wide.at[k, 8 : 8 + halo, :, cols], wide.at[k, 0:halo, :, cols],
-                wp_ss.at[k, s], wp_rs.at[k, s], dev(1, 0),
-            )
-            c.start()
-            wp.append(c)
-            c = rcopy(
-                wide.at[k, halo : 2 * halo, :, cols],
-                wide.at[k, halo + 8 : 2 * halo + 8, :, cols],
-                wm_ss.at[k, s], wm_rs.at[k, s], dev(-1, 0),
-            )
-            c.start()
-            wm.append(c)
-    sends += wp + wm + sp + sn
+            if k < nk - 1:
+                c = rcopy(
+                    wide.at[k, 8 : 8 + halo, :, cols], wide.at[k, 0:halo, :, cols],
+                    wp_ss.at[k, s], wp_rs.at[k, s], dev(1, 0),
+                )
+                c.start()
+                wp.append(c)
+                c = rcopy(
+                    wide.at[k, halo : 2 * halo, :, cols],
+                    wide.at[k, halo + 8 : 2 * halo + 8, :, cols],
+                    wm_ss.at[k, s], wm_rs.at[k, s], dev(-1, 0),
+                )
+                c.start()
+                wm.append(c)
+            else:
+                for i in range(halo):
+                    turned[i, :, cols] = wide[k, halo + jnp.where(even, halo - 1, 7) - i, :, cols]
+                land = pl.ds(jnp.where(even, 0, halo + 8), halo)
+                c = rcopy(
+                    turned.at[:, :, cols], wide.at[k, land, :, cols],
+                    wm_ss.at[k, s], wm_rs.at[k, s], image,
+                )
+                pl.when(has_image)(c.start)
+                wm.append(c)
+
+                @pl.when(own_image)
+                def _():
+                    wide[k, land, :, cols] = turned[:, :, cols]
+
+                c = rcopy(
+                    wide.at[k, pl.ds(jnp.where(even, 8, halo), halo), :, cols],
+                    wide.at[k, land, :, cols],
+                    wp_ss.at[k, s], wp_rs.at[k, s],
+                    {"gx": gx + jnp.where(even, 1, -1), "gy": gy, "gz": gz},
+                )
+                c.start()
+                wp.append(c)
+    sends += wp + wm[: 2 * nk - 2] + sp + sn
 
     for k in range(nk):
         sp[k].wait_recv()
@@ -350,8 +389,13 @@
             a = pltpu.roll(packs[slot], (PADL - 8 - 8 * x) % PADL, 1)
             b = pltpu.roll(packs[slot], 64 - 8 * x, 1)
             wide[k, w, :, ny:] = jnp.where(lane < 64, b, a)
-        for c in wp[2 * k : 2 * k + 2] + wm[2 * k : 2 * k + 2]:
+        for c in wp[2 * k : 2 * k + 2]:
             c.wait_recv()
+        for c in wm[2 * k : 2 * k + 2]:
+            if k < nk - 1:
+                c.wait_recv()
+            else:
+                pl.when(has_image)(c.wait)
 
         @pl.when(gx == 0)
         def _():
@@ -449,9 +493,7 @@
         ),
         in_specs=[
             hbm, hbm, hbm, hbm,
-            pl.BlockSpec(memory_space=pltpu.SMEM),
-            pl.BlockSpec(memory_space=pltpu.VMEM),
-            hbm,
+            hbm, hbm, hbm,
         ],
         out_specs=(vmem,) * 5,
         scratch_shapes=[
@@ -460,6 +502,7 @@
             v(3, rows, ny),
             pltpu.VMEM((rows, ny), jnp.int32),
             v(lrows, ny),
+            pltpu.SMEM(permittivity.shape, F32), pltpu.VMEM(design_mask.shape, jnp.int32),
             v(nchunk, 2, ZC, ny), v(nchunk, 2, ZC, ny),
             v(nchunk, 2, ZC, ny), v(nchunk, 2, ZC, ny),
             v(nchunk, 8, PADL), v(nchunk, 8, PADL),
@@ -470,9 +513,10 @@
             v(nk, 8, PADL), v(nk, 8, PADL),
             v(nk, 8, PADL), v(nk, 8, PADL),
             v(nk, 8, PADL), v(nk, 8, PADL), v(nk, 8, PADL), v(nk, 8, PADL), v(nk, 8, PADL),
-            dma((nt + 4,)),
+            v(halo, ZC, ny),
+            dma((nt + 6,)),
             dma((nchunk,)), dma((nchunk,)), dma((nchunk,)), dma((nchunk,)),
-            dma((nchunk,)), dma((nchunk,)), dma((nchunk,)), dma((nchunk,)),
+            dma((1,)), dma((1,)), dma((nchunk,)), dma((nchunk,)),
             dma((2,)), dma((2,)),
             dma((nk, 2)), dma((nk, 2)), dma((nk, 2)), dma((nk, 2)), dma((nk, 2)), dma((nk, 2)),
             dma((nk,)), dma((nk,)), dma((nk,)), dma((nk,)),

time: 35 us -> 33.6 us (0.960)
  Pallas kernels: 34.2 us -> 32.9 us
    pallas_call x1, Pallas kernels: 32.3 us -> 31 us  [on_device(): pl.pallas_call(functools.partial(kernel, sizes), out_shape=(v(3, rows, ny...]
where the time goes in v2:
time: 33.6 us; the launch traced here: 33.5 us
  Pallas kernels  32.9 us (98%)
  between operations  0.64 us (2%)
    pallas_call x1, Pallas kernels, on_device(): pl.pallas_call(functools.partial(kernel, sizes), out_shape=(v(3, rows, ny...  31 us
    pallas_call x1, Pallas kernels, on_device(): pl.pallas_call(finish, out_shape=(jax.ShapeDtypeStruct((3, rows, ny), F32...  1.92 us

profile of v2, /device:TPU:1, one launch (start us, length us, event | category | flops | bytes accessed | tf_op | source)
XLA Modules:
  0.0 33.5 jit_solution(15524363884304287870)
XLA Ops:
  0.6 31.0 %shard_map.102 = (f32[3,192,512]{2,1,0:T(8,128)S(1)}, f32[3,4,200,128]{3,2,1,0:T(8,128)S(1)}, f32[4,128,128]{2,1,0:T(8,128)S(1)}, f32[4,64,128]{2,1,0:T(8,128)S(1)}, f32[18,8,640]{2,1,0:T(8,128)S(1)}) custom-call(f32[3,192,512]{2,1,0:T(8,128)} %bitcast.9, f32[3,192,512]{2,1,0:T(8,128)} %bitcast.10, f32[3,192,512]{2,1,0:T(8,128)} %bitcast.11, ...), custom_call_target="tpu_custom_call" | custom-call | tf_op jit(solution)/shard_map/pallas_call | solution.py:485
  31.6 1.9 %shard_map.103 = (f32[3,192,512]{2,1,0:T(8,128)}, f32[3,192,512]{2,1,0:T(8,128)}, f32[128,512]{1,0:T(8,128)}, f32[128,512]{1,0:T(8,128)}) custom-call(f32[3,192,512]{2,1,0:T(8,128)S(1)} %get-tuple-element.13.en, f32[3,4,200,128]{3,2,1,0:T(8,128)S(1)} %get-tuple-element.14.hn, f32[4,128,128]{2,1,0:T(8,128)S(1)} %get-tuple-element.15.gt, ...), custom_call_target="tpu_custom_call" | custom-call | tf_op jit(solution)/shard_map/pallas_call | solution.py:532

commit v3 on v2

--- a/solution.py
+++ b/solution.py
@@ -30,15 +30,16 @@
     en, hn, gt, gf, last,
     ev, hv, fv, mv, gsv, perm_ref, mask_ref,
     xu_s, xu_r, xl_s, xl_r, yu_s, yu_r, yl_s, yl_r, zu_r, zl_r,
-    gsend, gmir, wide, el_s, er_s, el_r, er_r, q_s, q_m, sq, sq_p, sq_n, turned,
+    xe_s, xe_r, d2_s, d2_r, d3_r, zx_r, zy_r,
+    gsend, gmir, wide, el_s, er_s, el_r, er_r, turned,
     in_sem,
     xu_ss, xu_rs, xl_ss, xl_rs, yu_ss, yu_rs, yl_ss, yl_rs, z_ss, z_rs,
     m_ss, m_rs, wp_ss, wp_rs, wm_ss, wm_rs, el_ss, el_rs, er_ss, er_rs,
-    q_ss, q_rs, sp_ss, sp_rs, sn_ss, sn_rs,
+    d_ss, d_rs,
 ):
     ngx, ngy = sizes
     gx, gy, gz = lax.axis_index("gx"), lax.axis_index("gy"), lax.axis_index("gz")
-    ny = hv.shape[-1]
+    ny = fv.shape[-1]
     nchunk = m_hbm.shape[0] // (8 * ZC)
     rows = nchunk * ZC * 8
     half = ny // 2
@@ -60,7 +61,8 @@
     image = {"gx": lax.rem(image_at + ngx, ngx), "gy": gy, "gz": gz}
 
     barrier = pltpu.get_barrier_semaphore()
-    peers = [dev(-1, 0), dev(1, 0), dev(0, -1), dev(0, 1), mirror, zother]
+    peers = [dev(dx, dy) for dx in (-1, 0, 1) for dy in (-1, 0, 1) if (dx, dy) != (0, 0)]
+    peers += [mirror, zother]
     for peer in peers:
         pl.semaphore_signal(barrier, inc=1, device_id=peer, device_id_type=MESH)
 
@@ -97,19 +99,21 @@
         )
 
     c_e = [load(t, e_hbm.at[:, :, lanes(t)], ev.at[:, t, 0:rows, :]) for t in range(tiles)]
-    c_h = load(tiles, h_hbm, hv)
-    c_m = load(tiles + 1, m_hbm, mv)
-    c_f = load(tiles + 2, f_hbm, fv)
-    c_p = load(tiles + 4, perm_hbm, perm_ref)
-    c_k = load(tiles + 5, mask_hbm, mask_ref)
-    c_g = load(tiles + 3, gs_hbm, gsv)
+    c_h = [load(tiles + 5 + t, h_hbm.at[:, :, lanes(t)], hv.at[:, t]) for t in range(tiles)]
+    c_m = load(tiles, m_hbm, mv)
+    c_f = load(tiles + 1, f_hbm, fv)
+    c_p = load(tiles + 3, perm_hbm, perm_ref)
+    c_k = load(tiles + 4, mask_hbm, mask_ref)
+    c_g = load(tiles + 2, gs_hbm, gsv)
 
     sub = lax.broadcasted_iota(jnp.int32, (8, ny), 0)
     lane = lax.broadcasted_iota(jnp.int32, (8, PADL), 1)
     zero_tile = jnp.zeros((8, PADL), F32)
 
     low = gz == 0
-    zcs = [jnp.where(low, nchunk - 1 - k, k) for k in range(nchunk)]
+    high = jnp.logical_not(low)
+    zcs = [1, jnp.where(low, 2, 0), jnp.where(low, 0, 2)]
+    inner = ZC - 1
 
     def rows_at(z):
         return pl.multiple_of(z * 8, 8)
@@ -120,31 +124,65 @@
         )
 
     sends = []
+
+    def send(src, dst, sems, i, peer):
+        c = rcopy(src, dst, sems[0].at[i], sems[1].at[i], peer)
+        c.start()
+        sends.append(c)
+        return c
+
     for c in c_e:
         c.wait()
-    xu = []
+    ev[0:2, :, rows : rows + 8, :] = jnp.zeros((2, tiles, 8, PADL), F32)
+    bottom = lax.broadcasted_iota(jnp.int32, (8, PADL), 0) == 7
     for k in range(nchunk):
-        z0 = zcs[k] * ZC
+        r0 = rows_at(zcs[k] * ZC)
         for i, c in enumerate((1, 2)):
-            xu_s[k, i] = strided(ev, c, rows_at(z0))
+            xu_s[k, i] = strided(ev, c, r0)
+        d2_s[k] = ev[0, 0, pl.ds(r0 + 7, ZC, stride=8), :]
         acc = zero_tile
         for j in range(ZC):
-            r = rows_at(z0 + j)
             for i, c in enumerate((0, 2)):
-                tile = ev[c, 0, pl.ds(r, 8), :]
+                tile = ev[c, 0, pl.ds(rows_at(zcs[k] * ZC + j), 8), :]
                 at = 32 * i + j
                 acc = jnp.where(lane == at, pltpu.roll(tile, at, 1) if at else tile, acc)
         yu_s[k] = acc
+    for t in range(tiles):
+        xe_s[t : t + 1, :] = ev[2, t, 8 * inner : 8 * inner + 1, :]
+    for c in c_h:
+        c.wait()
+    for k in range(nchunk):
+        r0 = rows_at(zcs[k] * ZC)
+        ex, ey, ez = (strided(ev, c, r0 + 7) for c in range(3))
+        exz = strided(ev, 0, r0 + 15)
+        exy = pltpu.roll(jnp.concatenate([ex, zero_tile], 1), ny + PADL - 1, 1)[:, :ny]
+        xl_s[k, 0] = strided(hv, 1, r0 + 7) - COURANT * ((exz - ex) + ez)
+        xl_s[k, 1] = strided(hv, 2, r0 + 7) - COURANT * ((ex - exy) - ey)
+        acc = zero_tile
+        for j in range(ZC):
+            r = rows_at(zcs[k] * ZC + j)
+            ex, ey, ez = (ev[c, tiles - 1, pl.ds(r, 8), :] for c in range(3))
+            eyz = ev[1, tiles - 1, pl.ds(r + 8, 8), :]
+            eyx = jnp.where(bottom, 0.0, pltpu.roll(ey, 7, 0))
+            hz = hv[2, tiles - 1, pl.ds(r, 8), :] - COURANT * ((eyx - ey) + ex)
+            hx = hv[0, tiles - 1, pl.ds(r, 8), :] - COURANT * ((ey - eyz) - ez)
+            for i, f in enumerate((hz, hx, ey)):
+                at = 32 * i + j
+                acc = jnp.where(lane == at, pltpu.roll(f, at + 1, 1), acc)
+        yl_s[k] = acc
+
     pl.semaphore_wait(barrier, len(peers) + has_image.astype(jnp.int32))
-    yu = rcopy(yu_s, yu_r, yu_ss.at[0], yu_rs.at[0], dev(0, -1))
-    yu.start()
+    yu = send(yu_s, yu_r, (yu_ss, yu_rs), 0, dev(0, -1))
+    yl = send(yl_s, yl_r, (yl_ss, yl_rs), 0, dev(0, 1))
+    xe = send(xe_s, xe_r, (d_ss, d_rs), 0, dev(-1, 0))
+    d2 = send(d2_s, d2_r, (d_ss, d_rs), 1, dev(1, -1))
+    d3 = send(yl_s, d3_r, (d_ss, d_rs), 2, dev(-1, 1))
     zu = rcopy(ev.at[0:2, :, 0:8, :], zu_r, z_ss.at[0], z_rs.at[0], zother)
-    pl.when(jnp.logical_not(low))(zu.start)
+    pl.when(high)(zu.start)
+    xu, xl = [], []
     for k in range(nchunk):
-        c = rcopy(xu_s.at[k], xu_r.at[k], xu_ss.at[k], xu_rs.at[k], dev(-1, 0))
-        c.start()
-        xu.append(c)
-    sends += [yu] + xu
+        xu.append(send(xu_s.at[k], xu_r.at[k], (xu_ss, xu_rs), k, dev(-1, 0)))
+        xl.append(send(xl_s.at[k], xl_r.at[k], (xl_ss, xl_rs), k, dev(1, 0)))
 
     c_p.wait()
     c_k.wait()
@@ -158,95 +196,68 @@
     )
     inv = [1.0 / jnp.full((8, ny), perm_ref[i], F32) for i in range(perm_ref.shape[0])]
 
-    c_h.wait()
-
-    @pl.when(low)
-    def _():
-        zu.wait_recv()
-        ev[0:2, :, rows : rows + 8, :] = zu_r[...]
-
-    @pl.when(jnp.logical_not(low))
-    def _():
-        ev[0:2, :, rows : rows + 8, :] = jnp.zeros((2, tiles, 8, PADL), F32)
-
-    xl, yl = [], []
-    zl = None
-    for k in range(nchunk):
-        z0 = zcs[k] * ZC
-        if k == 0:
-            yu.wait_recv()
-        xu[k].wait_recv()
+    def shift_up_y(f, tile, at):
+        tile = pltpu.roll(tile, (PADL - at) % PADL, 1) if at else tile
+        return pltpu.roll(jnp.concatenate([f, tile], 1), ny + PADL - 1, 1)[:, :ny]
+
+    def shift_up_x(f, row):
+        return jnp.where(sub == 7, jnp.broadcast_to(row, (8, ny)), pltpu.roll(f, 7, 0))
+
+    def below_inner():
+        r = 8 * inner
+        ex, ey, ez = (plane(ev, c, r) for c in range(3))
+        exz, eyz = (plane(ev, c, r + 8) for c in range(2))
+        tile = jnp.where(gy == ngy - 1, 0.0, jnp.where(low, yu_r[2], yu_r[1]))
+        row = jnp.concatenate([xe_r[t : t + 1, :] for t in range(tiles)], 1)
+        ezy = shift_up_y(ez, tile, 32 + inner)
+        ezx = shift_up_x(ez, jnp.where(gx == ngx - 1, 0.0, row))
+        put(hn, plane(hv, 0, r) - COURANT * ((ezy - ez) - (eyz - ey)), 0, r + 8)
+        put(hn, plane(hv, 1, r) - COURANT * ((exz - ex) - (ezx - ez)), 1, r + 8)
+
+    def new_h(k):
         ytile = jnp.where(gy == ngy - 1, 0.0, yu_r[k])
         xu_r[k] = jnp.where(gx == ngx - 1, 0.0, xu_r[k])
-        acc = zero_tile
         for j in range(ZC):
-            r = rows_at(z0 + j)
+            r = rows_at(zcs[k] * ZC + j)
             ex, ey, ez = (plane(ev, c, r) for c in range(3))
             exz, eyz = (plane(ev, c, r + 8) for c in range(2))
-            hx, hy, hz = (hv[c, pl.ds(r, 8), :] for c in range(3))
-
-            def above_y(f, at):
-                tile = pltpu.roll(ytile, (PADL - at) % PADL, 1) if at else ytile
-                return pltpu.roll(jnp.concatenate([f, tile], 1), ny + PADL - 1, 1)[:, :ny]
-
-            def above_x(f, i):
-                row = jnp.broadcast_to(xu_r[k, i, j : j + 1, :], (8, ny))
-                return jnp.where(sub == 7, row, pltpu.roll(f, 7, 0))
-
-            exy, ezy = above_y(ex, j), above_y(ez, 32 + j)
-            eyx, ezx = above_x(ey, 0), above_x(ez, 1)
-            hxn = hx - COURANT * ((ezy - ez) - (eyz - ey))
-            hyn = hy - COURANT * ((exz - ex) - (ezx - ez))
-            hzn = hz - COURANT * ((eyx - ey) - (exy - ex))
-            for c, h in enumerate((hxn, hyn, hzn)):
-                put(hn, h, c, r + 8)
-            for i, h in enumerate((hzn, hxn)):
-                at = 32 * i + j
-                rolled = pltpu.roll(h[:, ny - PADL :], at + 1, 1)
-                acc = jnp.where(lane == at, rolled, acc)
-        yl_s[k] = acc
-        for i, c in enumerate((1, 2)):
-            xl_s[k, i] = strided(hn, c, rows_at(z0 + 1) + 7)
-        if k == 0:
-            zl = rcopy(hn.at[0:2, :, rows : rows + 8, :], zl_r, z_ss.at[1], z_rs.at[1], zother)
-        c = rcopy(yl_s.at[k], yl_r.at[k], yl_ss.at[k], yl_rs.at[k], dev(0, 1))
-        c.start()
-        yl.append(c)
-        c = rcopy(xl_s.at[k], xl_r.at[k], xl_ss.at[k], xl_rs.at[k], dev(1, 0))
-        c.start()
-        xl.append(c)
-        if k == 0:
-            pl.when(low)(zl.start)
-
-    sends += yl + xl
-
-    c_m.wait()
-    c_f.wait()
-    c_g.wait()
-
-    @pl.when(low)
-    def _():
-        hn[0, :, 0:8, :] = COURANT * ev[1, :, 0:8, :]
-        hn[1, :, 0:8, :] = -COURANT * ev[0, :, 0:8, :]
-
-    @pl.when(jnp.logical_not(low))
-    def _():
-        zl.wait_recv()
-        hn[0:2, :, 0:8, :] = zl_r[...]
+            hx, hy, hz = (plane(hv, c, r) for c in range(3))
+            exy, ezy = shift_up_y(ex, ytile, j), shift_up_y(ez, ytile, 32 + j)
+            eyx = shift_up_x(ey, xu_r[k, 0, j : j + 1, :])
+            ezx = shift_up_x(ez, xu_r[k, 1, j : j + 1, :])
+            put(hn, hx - COURANT * ((ezy - ez) - (eyz - ey)), 0, r + 8)
+            put(hn, hy - COURANT * ((exz - ex) - (ezx - ez)), 1, r + 8)
+            put(hn, hz - COURANT * ((eyx - ey) - (exy - ex)), 2, r + 8)
 
     sign = jnp.where(lane < 32, COURANT, -COURANT)
-    mir, el, er, qm = [], [], [], []
-    for k in range(nchunk):
-        z0 = zcs[k] * ZC
-        yl[k].wait_recv()
-        xl[k].wait_recv()
-        ytile = jnp.where(gy == 0, sign * yu_s[k], yl_r[k])
-        xl_r[k, 0] = jnp.where(gx == 0, COURANT * xu_s[k, 1], xl_r[k, 0])
-        xl_r[k, 1] = jnp.where(gx == 0, -COURANT * xu_s[k, 0], xl_r[k, 1])
+    subp = lax.broadcasted_iota(jnp.int32, (8, PADL), 0)
+
+    def new_e(k):
+        ytile = jnp.where(gy == 0, 0.0, yl_r[k])
+        beside = pltpu.roll(pltpu.roll(d3_r[k], 64, 1), 7, 0)
+        ytile = ytile - COURANT * jnp.where(
+            (subp == 7) & (lane < 32) & (gx != ngx - 1) & (gy != 0), beside, 0.0
+        )
+        row_y = jnp.where(gx == 0, 0.0, xl_r[k, 0])
+        row_z = jnp.where(gx == 0, 0.0, xl_r[k, 1])
+        corner = jnp.where(
+            (lane == PADL - 1) & (gx != 0) & (gy != ngy - 1), pltpu.roll(d2_r[k], PADL - 1, 1), 0.0
+        )
+        row_z = jnp.concatenate(
+            [row_z[:, : ny - PADL], row_z[:, ny - PADL :] + COURANT * corner], 1
+        )
+        if k == 1:
+            over = pltpu.roll(zy_r[...], 40, 1)
+            ytile = ytile + COURANT * jnp.where((lane == 39) & low & (gy != 0), over, 0.0)
+            over = jnp.concatenate([zx_r[t] for t in range(tiles)], 1)
+            row_y = row_y - COURANT * jnp.where((sub == 7) & low & (gx != 0), over, 0.0)
+        ytile = ytile + sign * yu_s[k]
+        xl_r[k, 0] = row_y + COURANT * xu_s[k, 1]
+        xl_r[k, 1] = row_z - COURANT * xu_s[k, 0]
         design = k < nchunk - 1
-        l0 = (z0 - jnp.where(low, ZC, 0)) if design else None
+        l0 = zcs[k] * ZC - jnp.where(low, ZC, 0) if design else None
         for j in range(ZC):
-            r = rows_at(z0 + j)
+            r = rows_at(zcs[k] * ZC + j)
             hx, hy, hz = (plane(hn, c, r + 8) for c in range(3))
             hxz, hyz = (plane(hn, c, r) for c in range(2))
 
@@ -280,63 +291,97 @@
             if design:
                 lr = rows_at(l0 + j)
                 put(gt, gsv[pl.ds(lr, 8), :] + mask * dot, lr)
-        if design:
-            left, right = zero_tile, zero_tile
-            for x in range(8):
-                g = strided(gt, rows_at(l0) + x)
-                gsend[k, x] = g
-                here = (lane // 8) == x
-                t = g[:, :PADL]
-                left = jnp.where(here, pltpu.roll(t, 8 * x, 1) if x else t, left)
-                right = jnp.where(here, pltpu.roll(g[:, ny - PADL :], 8 * x + 8, 1), right)
-            er_s[k] = right
-            el_s[k] = left
-            c = rcopy(er_s.at[k], el_r.at[k], el_ss.at[k], el_rs.at[k], dev(0, 1))
-            c.start()
-            el.append(c)
-            c = rcopy(el_s.at[k], er_r.at[k], er_ss.at[k], er_rs.at[k], dev(0, -1))
-            c.start()
-            er.append(c)
-            for s in range(2):
-                cols = slice(s * half, (s + 1) * half)
-                c = rcopy(
-                    gsend.at[k, :, :, cols], gmir.at[k, :, :, cols],
-                    m_ss.at[k, s], m_rs.at[k, s], mirror,
-                )
-                c.start()
-                mir.append(c)
-    for k in range(nchunk - 1):
-        el[k].wait_recv()
-        er[k].wait_recv()
-        beyond_left = jnp.where(gy == 0, 0.0, el_r[k])
-        beyond_right = jnp.where(gy == ngy - 1, 0.0, er_r[k])
-        q_s[k] = jnp.where(lane < 64, beyond_left, pltpu.roll(beyond_right, 64, 1))
-        c = rcopy(q_s.at[k], q_m.at[k], q_ss.at[k], q_rs.at[k], mirror)
-        c.start()
-        qm.append(c)
-    sends += mir + el + er + qm
+        return l0
+
+    mir = []
+
+    def send_gradient(k, l0):
+        for x in range(8):
+            gsend[k, x] = strided(gt, rows_at(l0) + x)
+        for s in range(2):
+            cols = slice(s * half, (s + 1) * half)
+            mir.append(
+                send(gsend.at[k, :, :, cols], gmir.at[k, :, :, cols], (m_ss.at[k], m_rs.at[k]), s, mirror)
+            )
+
+    zl = rcopy(hn.at[0:2, :, rows : rows + 8, :], zl_r, z_ss.at[1], z_rs.at[1], zother)
+    zx = rcopy(zu_r.at[0], zx_r, d_ss.at[3], d_rs.at[3], dev(1, 0))
+    zy = rcopy(zu_r.at[1, tiles - 1], zy_r, d_ss.at[4], d_rs.at[4], dev(0, 1))
+
+    yu.wait_recv()
+    xe.wait_recv()
+    below_inner()
+    xu[0].wait_recv()
+    new_h(0)
+
+    @pl.when(low)
+    def _():
+        zu.wait_recv()
+        zx.start()
+        zy.start()
+        ev[0:2, :, rows : rows + 8, :] = zu_r[...]
+        hn[0, :, 0:8, :] = COURANT * ev[1, :, 0:8, :]
+        hn[1, :, 0:8, :] = -COURANT * ev[0, :, 0:8, :]
+
+    xu[1].wait_recv()
+    new_h(1)
+    pl.when(low)(zl.start)
+
+    c_m.wait()
+    c_f.wait()
+    c_g.wait()
+    yl.wait_recv()
+    d2.wait_recv()
+    d3.wait_recv()
+    xl[0].wait_recv()
+    send_gradient(0, new_e(0))
+
+    @pl.when(low)
+    def _():
+        zx.wait_recv()
+        zy.wait_recv()
+
+    @pl.when(high)
+    def _():
+        zx_r[...] = jnp.zeros((tiles, 8, PADL), F32)
+        zy_r[...] = zero_tile
+        zl.wait_recv()
+        hn[0:2, :, 0:8, :] = zl_r[...]
+
+    xl[1].wait_recv()
+    send_gradient(1, new_e(1))
+
+    xu[2].wait_recv()
+    new_h(2)
+    xl[2].wait_recv()
+    new_e(2)
 
     halo = RADIUS - 1
     nk = nchunk - 1
-    wp, wm, sp, sn = [], [], [], []
+    wp, wm, el, er = [], [], [], []
     for k in range(nk):
-        qm[k].wait_recv()
-        flipped = zero_tile
-        for x in range(8):
-            here = ((lane // 8) % 8) == x
-            flipped = jnp.where(here, pltpu.roll(q_m[k], (8 * (2 * x - 7)) % PADL, 1), flipped)
-        sq[k] = q_s[k] + flipped
-        c = rcopy(sq.at[k], sq_p.at[k], sp_ss.at[k], sp_rs.at[k], dev(1, 0))
-        c.start()
-        sp.append(c)
-        c = rcopy(sq.at[k], sq_n.at[k], sn_ss.at[k], sn_rs.at[k], dev(-1, 0))
-        c.start()
-        sn.append(c)
         for s in range(2):
             cols = slice(s * half, (s + 1) * half)
             mir[2 * k + s].wait_recv()
             for x in range(8):
                 wide[k, halo + x, :, cols] = gsend[k, x, :, cols] + gmir[k, 7 - x, :, cols]
+            acc = zero_tile
+            for x in range(8):
+                edge = wide[k, halo + x, :, 0:PADL] if s == 0 else wide[k, halo + x, :, ny - PADL : ny]
+                at = (8 * x + 8 * s) % PADL
+                acc = jnp.where((lane // 8) == x, pltpu.roll(edge, at, 1) if at else edge, acc)
+            if s == 0:
+                el_s[k] = acc
+                for d in (0, 1, -1):
+                    er.append(
+                        send(el_s.at[k], er_r.at[k, 1 - d], (er_ss.at[k], er_rs.at[k]), 1 - d, dev(d, -1))
+                    )
+            else:
+                er_s[k] = acc
+                for d in (0, 1, -1):
+                    el.append(
+                        send(er_s.at[k], el_r.at[k, 1 - d], (el_ss.at[k], el_rs.at[k]), 1 - d, dev(d, 1))
+                    )
             if k < nk - 1:
                 c = rcopy(
                     wide.at[k, 8 : 8 + halo, :, cols], wide.at[k, 0:halo, :, cols],
@@ -374,20 +419,24 @@
                 )
                 c.start()
                 wp.append(c)
-    sends += wp + wm[: 2 * nk - 2] + sp + sn
+    sends += wp + wm[: 2 * nk - 2]
 
     for k in range(nk):
-        sp[k].wait_recv()
-        sn[k].wait_recv()
-        packs = (
-            jnp.where(gx == 0, 0.0, sq_p[k]),
-            sq[k],
-            jnp.where(gx == ngx - 1, 0.0, sq_n[k]),
-        )
+        for c in el[3 * k : 3 * k + 3] + er[3 * k : 3 * k + 3]:
+            c.wait_recv()
+        packs = []
+        for slot in range(3):
+            gone = (gx == 0, gx < 0, gx == ngx - 1)[slot]
+            packs.append(
+                (
+                    jnp.where((gy == 0) | gone, 0.0, el_r[k, slot]),
+                    jnp.where((gy == ngy - 1) | gone, 0.0, er_r[k, slot]),
+                )
+            )
         for w in range(8 + 2 * halo):
             slot, x = (w - halo + 8) // 8, (w - halo) % 8
-            a = pltpu.roll(packs[slot], (PADL - 8 - 8 * x) % PADL, 1)
-            b = pltpu.roll(packs[slot], 64 - 8 * x, 1)
+            a = pltpu.roll(packs[slot][0], (PADL - 8 - 8 * x) % PADL, 1)
+            b = pltpu.roll(packs[slot][1], PADL - 8 * x, 1) if x else packs[slot][1]
             wide[k, w, :, ny:] = jnp.where(lane < 64, b, a)
         for c in wp[2 * k : 2 * k + 2]:
             c.wait_recv()
@@ -410,8 +459,12 @@
         else:
             last[...] = wide[k]
 
-    pl.when(low)(zl.wait_send)
-    pl.when(jnp.logical_not(low))(zu.wait_send)
+    @pl.when(low)
+    def _():
+        for c in (zl, zx, zy):
+            c.wait_send()
+
+    pl.when(high)(zu.wait_send)
     for c in sends:
         c.wait_send()
 
@@ -457,7 +510,7 @@
         outs.append(c)
 
     n = 8 * ZC
-    first = pl.multiple_of(jnp.where(low, n, 0), n)
+    first = pl.multiple_of(jnp.where(low, 0, n), n)
     store(en, eo)
     for t in range(tiles):
         cols = slice(t * PADL, (t + 1) * PADL)
@@ -498,7 +551,7 @@
         out_specs=(vmem,) * 5,
         scratch_shapes=[
             v(3, nt, rows + 8, PADL),
-            v(3, rows, ny),
+            v(3, nt, rows, PADL),
             v(3, rows, ny),
             pltpu.VMEM((rows, ny), jnp.int32),
             v(lrows, ny),
@@ -508,19 +561,20 @@
             v(nchunk, 8, PADL), v(nchunk, 8, PADL),
             v(nchunk, 8, PADL), v(nchunk, 8, PADL),
             v(2, nt, 8, PADL), v(2, nt, 8, PADL),
+            v(8, PADL), v(8, PADL), v(nchunk, 8, PADL), v(nchunk, 8, PADL), v(nchunk, 8, PADL),
+            v(nt, 8, PADL), v(8, PADL),
             v(nk, 8, ZC, ny), v(nk, 8, ZC, ny),
             v(nk, 8 + 2 * halo, ZC, ny + PADL),
             v(nk, 8, PADL), v(nk, 8, PADL),
-            v(nk, 8, PADL), v(nk, 8, PADL),
-            v(nk, 8, PADL), v(nk, 8, PADL), v(nk, 8, PADL), v(nk, 8, PADL), v(nk, 8, PADL),
+            v(nk, 3, 8, PADL), v(nk, 3, 8, PADL),
             v(halo, ZC, ny),
-            dma((nt + 6,)),
+            dma((2 * nt + 5,)),
             dma((nchunk,)), dma((nchunk,)), dma((nchunk,)), dma((nchunk,)),
-            dma((1,)), dma((1,)), dma((nchunk,)), dma((nchunk,)),
+            dma((1,)), dma((1,)), dma((1,)), dma((1,)),
             dma((2,)), dma((2,)),
             dma((nk, 2)), dma((nk, 2)), dma((nk, 2)), dma((nk, 2)), dma((nk, 2)), dma((nk, 2)),
-            dma((nk,)), dma((nk,)), dma((nk,)), dma((nk,)),
-            dma((nk,)), dma((nk,)), dma((nk,)), dma((nk,)), dma((nk,)), dma((nk,)),
+            dma((nk, 3)), dma((nk, 3)), dma((nk, 3)), dma((nk, 3)),
+            dma((5,)), dma((5,)),
         ],
         compiler_params=pltpu.CompilerParams(
             collective_id=0, has_side_effects=True, vmem_limit_bytes=63_500_000

time: 33.6 us -> 32.3 us (0.961)
  Pallas kernels: 32.9 us -> 31.5 us
    pallas_call x1, Pallas kernels: 31 us -> 29.6 us  [on_device(): pl.pallas_call(functools.partial(kernel, sizes), out_shape=(v(3, rows, ny...]
where the time goes in v3:
time: 32.3 us; the launch traced here: 32.1 us
  Pallas kernels  31.5 us (98%)
  between operations  0.64 us (2%)
    pallas_call x1, Pallas kernels, on_device(): pl.pallas_call(functools.partial(kernel, sizes), out_shape=(v(3, rows, ny...  29.6 us
    pallas_call x1, Pallas kernels, on_device(): pl.pallas_call(finish, out_shape=(jax.ShapeDtypeStruct((3, rows, ny), F32...  1.92 us

profile of v3, /device:TPU:1, one launch (start us, length us, event | category | flops | bytes accessed | tf_op | source)
XLA Modules:
  0.0 32.1 jit_solution(17383026919814058998)
XLA Ops:
  0.6 29.6 %shard_map.102 = (f32[3,192,512]{2,1,0:T(8,128)S(1)}, f32[3,4,200,128]{3,2,1,0:T(8,128)S(1)}, f32[4,128,128]{2,1,0:T(8,128)S(1)}, f32[4,64,128]{2,1,0:T(8,128)S(1)}, f32[18,8,640]{2,1,0:T(8,128)S(1)}) custom-call(f32[3,192,512]{2,1,0:T(8,128)} %bitcast.9, f32[3,192,512]{2,1,0:T(8,128)} %bitcast.10, f32[3,192,512]{2,1,0:T(8,128)} %bitcast.11, ...), custom_call_target="tpu_custom_call" | custom-call | tf_op jit(solution)/shard_map/pallas_call | solution.py:538
  30.2 1.9 %shard_map.103 = (f32[3,192,512]{2,1,0:T(8,128)}, f32[3,192,512]{2,1,0:T(8,128)}, f32[128,512]{1,0:T(8,128)}, f32[128,512]{1,0:T(8,128)}) custom-call(f32[3,192,512]{2,1,0:T(8,128)S(1)} %get-tuple-element.13.en, f32[3,4,200,128]{3,2,1,0:T(8,128)S(1)} %get-tuple-element.14.hn, f32[4,128,128]{2,1,0:T(8,128)S(1)} %get-tuple-element.15.gt, ...), custom_call_target="tpu_custom_call" | custom-call | tf_op jit(solution)/shard_map/pallas_call | solution.py:586

commit v4 on v3

--- a/solution.py
+++ b/solution.py
@@ -29,7 +29,7 @@
     e_hbm, h_hbm, f_hbm, m_hbm, perm_hbm, mask_hbm, gs_hbm,
     en, hn, gt, gf, last,
     ev, hv, fv, mv, gsv, perm_ref, mask_ref,
-    xu_s, xu_r, xl_s, xl_r, yu_s, yu_r, yl_s, yl_r, zu_r, zl_r,
+    xu_s, xu_r, xl_s, xl_r, yu_s, yu_r, yl_s, yl_r, zu_r, zl_s, zl_r,
     xe_s, xe_r, d2_s, d2_r, d3_r, zx_r, zy_r,
     gsend, gmir, wide, el_s, er_s, el_r, er_r, turned,
     in_sem,
@@ -55,6 +55,7 @@
     zother = {"gx": gx, "gy": gy, "gz": 1 - gz}
 
     even = lax.rem(gx, 2) == 0
+    core = lax.rem(gy, 2)
     image_at = jnp.where(even, ngx, ngx - 2) - gx
     own_image = image_at == gx
     has_image = (gx != 0) & (gx != ngx - 1) & jnp.logical_not(own_image)
@@ -149,15 +150,43 @@
         yu_s[k] = acc
     for t in range(tiles):
         xe_s[t : t + 1, :] = ev[2, t, 8 * inner : 8 * inner + 1, :]
-    for c in c_h:
-        c.wait()
-    for k in range(nchunk):
+    pl.semaphore_wait(barrier, len(peers) + has_image.astype(jnp.int32))
+    zu = rcopy(ev.at[0:2, :, 0:8, :], zu_r, z_ss.at[0], z_rs.at[0], zother)
+    zl = rcopy(zl_s, zl_r, z_ss.at[1], z_rs.at[1], zother)
+    pl.when(high)(zu.start)
+    yu = send(yu_s, yu_r, (yu_ss, yu_rs), 0, dev(0, -1))
+    xe = send(xe_s, xe_r, (d_ss, d_rs), 0, dev(-1, 0))
+    d2 = send(d2_s, d2_r, (d_ss, d_rs), 1, dev(1, -1))
+    xu, xl = [], []
+
+    def send_xu(k):
+        xu.append(send(xu_s.at[k], xu_r.at[k], (xu_ss, xu_rs), k, dev(-1, 0)))
+
+    def send_xl(k):
         r0 = rows_at(zcs[k] * ZC)
         ex, ey, ez = (strided(ev, c, r0 + 7) for c in range(3))
         exz = strided(ev, 0, r0 + 15)
         exy = pltpu.roll(jnp.concatenate([ex, zero_tile], 1), ny + PADL - 1, 1)[:, :ny]
         xl_s[k, 0] = strided(hv, 1, r0 + 7) - COURANT * ((exz - ex) + ez)
         xl_s[k, 1] = strided(hv, 2, r0 + 7) - COURANT * ((ex - exy) - ey)
+        xl.append(send(xl_s.at[k], xl_r.at[k], (xl_ss, xl_rs), k, dev(1, 0)))
+
+    send_xu(0)
+    for c in c_h:
+        c.wait()
+
+    @pl.when(low)
+    def _():
+        r = rows - 8
+        ex, ey, ez = (plane(ev, c, r) for c in range(3))
+        ezy = pltpu.roll(jnp.concatenate([ez, zero_tile], 1), ny + PADL - 1, 1)[:, :ny]
+        ezx = jnp.where(sub == 7, 0.0, pltpu.roll(ez, 7, 0))
+        put(zl_s, plane(hv, 0, r) - COURANT * ((ezy - ez) + ey), 0, 0)
+        put(zl_s, plane(hv, 1, r) - COURANT * ((ez - ezx) - ex), 1, 0)
+        put(zl_s, ez, 2, 0)
+        zl.start()
+
+    for k in range(nchunk):
         acc = zero_tile
         for j in range(ZC):
             r = rows_at(zcs[k] * ZC + j)
@@ -170,19 +199,12 @@
                 at = 32 * i + j
                 acc = jnp.where(lane == at, pltpu.roll(f, at + 1, 1), acc)
         yl_s[k] = acc
-
-    pl.semaphore_wait(barrier, len(peers) + has_image.astype(jnp.int32))
-    yu = send(yu_s, yu_r, (yu_ss, yu_rs), 0, dev(0, -1))
     yl = send(yl_s, yl_r, (yl_ss, yl_rs), 0, dev(0, 1))
-    xe = send(xe_s, xe_r, (d_ss, d_rs), 0, dev(-1, 0))
-    d2 = send(d2_s, d2_r, (d_ss, d_rs), 1, dev(1, -1))
     d3 = send(yl_s, d3_r, (d_ss, d_rs), 2, dev(-1, 1))
-    zu = rcopy(ev.at[0:2, :, 0:8, :], zu_r, z_ss.at[0], z_rs.at[0], zother)
-    pl.when(high)(zu.start)
-    xu, xl = [], []
-    for k in range(nchunk):
-        xu.append(send(xu_s.at[k], xu_r.at[k], (xu_ss, xu_rs), k, dev(-1, 0)))
-        xl.append(send(xl_s.at[k], xl_r.at[k], (xl_ss, xl_rs), k, dev(1, 0)))
+    send_xl(0)
+    for k in range(1, nchunk):
+        send_xu(k)
+        send_xl(k)
 
     c_p.wait()
     c_k.wait()
@@ -304,28 +326,16 @@
                 send(gsend.at[k, :, :, cols], gmir.at[k, :, :, cols], (m_ss.at[k], m_rs.at[k]), s, mirror)
             )
 
-    zl = rcopy(hn.at[0:2, :, rows : rows + 8, :], zl_r, z_ss.at[1], z_rs.at[1], zother)
-    zx = rcopy(zu_r.at[0], zx_r, d_ss.at[3], d_rs.at[3], dev(1, 0))
-    zy = rcopy(zu_r.at[1, tiles - 1], zy_r, d_ss.at[4], d_rs.at[4], dev(0, 1))
+    zx_up = rcopy(zu_r.at[0], zx_r, d_ss.at[3], d_rs.at[3], dev(1, 0))
+    zy_up = rcopy(zu_r.at[1, tiles - 1], zy_r, d_ss.at[4], d_rs.at[4], dev(0, 1))
+    zx_dn = rcopy(zl_r.at[2], zx_r, d_ss.at[3], d_rs.at[3], dev(-1, 0))
+    zy_dn = rcopy(zl_r.at[2, 0], zy_r, d_ss.at[4], d_rs.at[4], dev(0, -1))
 
     yu.wait_recv()
     xe.wait_recv()
     below_inner()
     xu[0].wait_recv()
     new_h(0)
-
-    @pl.when(low)
-    def _():
-        zu.wait_recv()
-        zx.start()
-        zy.start()
-        ev[0:2, :, rows : rows + 8, :] = zu_r[...]
-        hn[0, :, 0:8, :] = COURANT * ev[1, :, 0:8, :]
-        hn[1, :, 0:8, :] = -COURANT * ev[0, :, 0:8, :]
-
-    xu[1].wait_recv()
-    new_h(1)
-    pl.when(low)(zl.start)
 
     c_m.wait()
     c_f.wait()
@@ -334,21 +344,46 @@
     d2.wait_recv()
     d3.wait_recv()
     xl[0].wait_recv()
-    send_gradient(0, new_e(0))
+    layer = new_e(0)
 
     @pl.when(low)
     def _():
-        zx.wait_recv()
-        zy.wait_recv()
+        zu.wait_recv()
+        zx_up.start()
+        zy_up.start()
+        ev[0:2, :, rows : rows + 8, :] = zu_r[...]
 
     @pl.when(high)
     def _():
-        zx_r[...] = jnp.zeros((tiles, 8, PADL), F32)
-        zy_r[...] = zero_tile
         zl.wait_recv()
-        hn[0:2, :, 0:8, :] = zl_r[...]
-
+        zx_dn.start()
+        zy_dn.start()
+
+    send_gradient(0, layer)
+
+    xu[1].wait_recv()
+    new_h(1)
     xl[1].wait_recv()
+    zx_up.wait_recv()
+    zy_up.wait_recv()
+    up_y, up_x = COURANT * ev[1, :, 0:8, :], COURANT * ev[0, :, 0:8, :]
+
+    @pl.when(low)
+    def _():
+        hn[0, :, 0:8, :] = up_y
+        hn[1, :, 0:8, :] = -up_x
+
+    @pl.when(high)
+    def _():
+        hn[0, :, 0:8, :] = zl_r[0] + up_y
+        corner = jnp.where(
+            (lane == PADL - 1) & (gy != ngy - 1), pltpu.roll(zy_r[...], PADL - 1, 1), 0.0
+        )
+        hn[0, tiles - 1, 0:8, :] = hn[0, tiles - 1, 0:8, :] - COURANT * corner
+        for t in range(tiles):
+            edge = jnp.where(bottom & (gx != ngx - 1), pltpu.roll(zx_r[t], 7, 0), 0.0)
+            hn[1, t, 0:8, :] = zl_r[1, t] - up_x[t] + COURANT * edge
+
     send_gradient(1, new_e(1))
 
     xu[2].wait_recv()
@@ -373,44 +408,32 @@
             if s == 0:
                 el_s[k] = acc
                 for d in (0, 1, -1):
-                    er.append(
-                        send(el_s.at[k], er_r.at[k, 1 - d], (er_ss.at[k], er_rs.at[k]), 1 - d, dev(d, -1))
-                    )
+                    rcopy(el_s.at[k], er_r.at[k, 1 - d], er_ss.at[k], er_rs.at[k], dev(d, -1)).start()
+                er.append(rcopy(er_r.at[k], er_r.at[k], er_ss.at[k], er_rs.at[k], dev(0, -1)))
             else:
                 er_s[k] = acc
                 for d in (0, 1, -1):
-                    el.append(
-                        send(er_s.at[k], el_r.at[k, 1 - d], (el_ss.at[k], el_rs.at[k]), 1 - d, dev(d, 1))
+                    rcopy(er_s.at[k], el_r.at[k, 1 - d], el_ss.at[k], el_rs.at[k], dev(d, 1)).start()
+                el.append(rcopy(el_r.at[k], el_r.at[k], el_ss.at[k], el_rs.at[k], dev(0, 1)))
+            if k < nk - 1:
+                for up, ss, rs, out in ((core == 0, wp_ss, wp_rs, wp), (core == 1, wm_ss, wm_rs, wm)):
+                    c = rcopy(
+                        wide.at[k, pl.ds(jnp.where(up, 8, halo), halo), :, cols],
+                        wide.at[k, pl.ds(jnp.where(up, 0, halo + 8), halo), :, cols],
+                        ss.at[k, s], rs.at[k, s],
+                        {"gx": lax.rem(gx + jnp.where(up, 1, ngx - 1), ngx), "gy": gy, "gz": gz},
                     )
-            if k < nk - 1:
-                c = rcopy(
-                    wide.at[k, 8 : 8 + halo, :, cols], wide.at[k, 0:halo, :, cols],
-                    wp_ss.at[k, s], wp_rs.at[k, s], dev(1, 0),
-                )
-                c.start()
-                wp.append(c)
-                c = rcopy(
-                    wide.at[k, halo : 2 * halo, :, cols],
-                    wide.at[k, halo + 8 : 2 * halo + 8, :, cols],
-                    wm_ss.at[k, s], wm_rs.at[k, s], dev(-1, 0),
-                )
-                c.start()
-                wm.append(c)
+                    c.start()
+                    out.append(c)
             else:
                 for i in range(halo):
                     turned[i, :, cols] = wide[k, halo + jnp.where(even, halo - 1, 7) - i, :, cols]
                 land = pl.ds(jnp.where(even, 0, halo + 8), halo)
-                c = rcopy(
+                c_image = rcopy(
                     turned.at[:, :, cols], wide.at[k, land, :, cols],
                     wm_ss.at[k, s], wm_rs.at[k, s], image,
                 )
-                pl.when(has_image)(c.start)
-                wm.append(c)
-
-                @pl.when(own_image)
-                def _():
-                    wide[k, land, :, cols] = turned[:, :, cols]
-
+                pl.when(has_image & (core == 0))(c_image.start)
                 c = rcopy(
                     wide.at[k, pl.ds(jnp.where(even, 8, halo), halo), :, cols],
                     wide.at[k, land, :, cols],
@@ -418,12 +441,19 @@
                     {"gx": gx + jnp.where(even, 1, -1), "gy": gy, "gz": gz},
                 )
                 c.start()
+                pl.when(has_image & (core == 1))(c_image.start)
                 wp.append(c)
-    sends += wp + wm[: 2 * nk - 2]
+                wm.append(c_image)
+
+                @pl.when(own_image)
+                def _():
+                    wide[k, land, :, cols] = turned[:, :, cols]
+
+    sends += wp + wm[: 2 * nk - 2] + el + er
 
     for k in range(nk):
-        for c in el[3 * k : 3 * k + 3] + er[3 * k : 3 * k + 3]:
-            c.wait_recv()
+        el[k].wait_recv()
+        er[k].wait_recv()
         packs = []
         for slot in range(3):
             gone = (gx == 0, gx < 0, gx == ngx - 1)[slot]
@@ -459,11 +489,9 @@
         else:
             last[...] = wide[k]
 
-    @pl.when(low)
-    def _():
-        for c in (zl, zx, zy):
-            c.wait_send()
-
+    zx_up.wait_send()
+    zy_up.wait_send()
+    pl.when(low)(zl.wait_send)
     pl.when(high)(zu.wait_send)
     for c in sends:
         c.wait_send()
@@ -560,7 +588,7 @@
             v(nchunk, 2, ZC, ny), v(nchunk, 2, ZC, ny),
             v(nchunk, 8, PADL), v(nchunk, 8, PADL),
             v(nchunk, 8, PADL), v(nchunk, 8, PADL),
-            v(2, nt, 8, PADL), v(2, nt, 8, PADL),
+            v(2, nt, 8, PADL), v(3, nt, 8, PADL), v(3, nt, 8, PADL),
             v(8, PADL), v(8, PADL), v(nchunk, 8, PADL), v(nchunk, 8, PADL), v(nchunk, 8, PADL),
             v(nt, 8, PADL), v(8, PADL),
             v(nk, 8, ZC, ny), v(nk, 8, ZC, ny),
@@ -573,7 +601,7 @@
             dma((1,)), dma((1,)), dma((1,)), dma((1,)),
             dma((2,)), dma((2,)),
             dma((nk, 2)), dma((nk, 2)), dma((nk, 2)), dma((nk, 2)), dma((nk, 2)), dma((nk, 2)),
-            dma((nk, 3)), dma((nk, 3)), dma((nk, 3)), dma((nk, 3)),
+            dma((nk,)), dma((nk,)), dma((nk,)), dma((nk,)),
             dma((5,)), dma((5,)),
         ],
         compiler_params=pltpu.CompilerParams(

time: 32.3 us -> 32.3 us (level)
  no operation moved by 1% of the time
where the time goes in v4:
time: 32.3 us; the launch traced here: 32.2 us
  Pallas kernels  31.6 us (98%)
  between operations  0.64 us (2%)
    pallas_call x1, Pallas kernels, on_device(): pl.pallas_call(functools.partial(kernel, sizes), out_shape=(v(3, rows, ny...  29.7 us
    pallas_call x1, Pallas kernels, on_device(): pl.pallas_call(finish, out_shape=(jax.ShapeDtypeStruct((3, rows, ny), F32...  1.92 us

profile of v4, /device:TPU:1, one launch (start us, length us, event | category | flops | bytes accessed | tf_op | source)
XLA Modules:
  0.0 32.2 jit_solution(13778891029044652701)
XLA Ops:
  0.6 29.7 %shard_map.102 = (f32[3,192,512]{2,1,0:T(8,128)S(1)}, f32[3,4,200,128]{3,2,1,0:T(8,128)S(1)}, f32[4,128,128]{2,1,0:T(8,128)S(1)}, f32[4,64,128]{2,1,0:T(8,128)S(1)}, f32[18,8,640]{2,1,0:T(8,128)S(1)}) custom-call(f32[3,192,512]{2,1,0:T(8,128)} %bitcast.9, f32[3,192,512]{2,1,0:T(8,128)} %bitcast.10, f32[3,192,512]{2,1,0:T(8,128)} %bitcast.11, ...), custom_call_target="tpu_custom_call" | custom-call | tf_op jit(solution)/shard_map/pallas_call | solution.py:566
  30.3 1.9 %shard_map.103 = (f32[3,192,512]{2,1,0:T(8,128)}, f32[3,192,512]{2,1,0:T(8,128)}, f32[128,512]{1,0:T(8,128)}, f32[128,512]{1,0:T(8,128)}) custom-call(f32[3,192,512]{2,1,0:T(8,128)S(1)} %get-tuple-element.13.en, f32[3,4,200,128]{3,2,1,0:T(8,128)S(1)} %get-tuple-element.14.hn, f32[4,128,128]{2,1,0:T(8,128)S(1)} %get-tuple-element.15.gt, ...), custom_call_target="tpu_custom_call" | custom-call | tf_op jit(solution)/shard_map/pallas_call | solution.py:614
